TPU v7x, 32 devices: a whole 2x2x4 slice. The times are simulated.
32 devices in a mesh: grp: 2 (over x), chan: 16 (over z, y, core).
Axes of the slice: x: 2, y: 2, z: 4, core: 2. Of those that a mesh axis runs over, the one named last changes fastest.
Arguments:
- samples: bfloat16 [32, 16, 256, 1024], P(('grp', 'chan')), parts along dimension 0, may hold values from -6 to 6
- fir: float32 [16, 1024], replicated, may hold values from -1.5 to 1.5
- chan_assign: int32 [256], replicated, may hold values from 0 to 511, as said below
- input_order: int32 [1024], replicated, may hold values from 0 to 1023, each once
Outputs:
- vis: bfloat16 [512, 1024, 1024], P(('grp', 'chan')), parts along dimension 0
There are 2 independent parts, one for each index of `grp`. A program takes and returns all parts, laid end to end along the dimension named above; an argument that names none is the same for every part. Nothing has to cross between parts.
Inputs may be any that keep to these rules, and one draw needn't show every extreme that they name: `chan_assign`: distinct transform bins; bin 0 and bin 1024 // 2 - 1 are always among them. `input_order`: each input number once.
All inputs are finite; a program needn't handle non-finite values.
Results may differ from a plain program's by a relative error of at most 0.0074.
Values may be sent and summed in bfloat16 or wider, within the bound.
No kernel may reach another device: no remote copies, remote signals or barrier semaphores. Data moves between devices by JAX's collectives and lax.ppermute only.
A program may use at most 256 MiB of HBM per device.

v0:
```python
import math

import jax
import jax.numpy as jnp
from jax import lax
from jax.sharding import PartitionSpec as P

QUART = 4


def shifted(value, axis, steps):
    count = lax.axis_size(axis)
    initial, last = (max(0, -steps), min(count, count - steps))
    return lax.ppermute(value, axis, [(source, source + steps) for source in range(initial, last)])


def make_table(chan_assign, frame_len):
    samples_index = jnp.arange(frame_len, dtype=jnp.int32)
    phase_index = chan_assign[:, None] * samples_index[None, :] % frame_len
    angles = phase_index.astype(jnp.float32) * (2.0 * math.pi / frame_len)
    norm_scale = 1.0 / math.sqrt(frame_len)
    return jnp.stack([jnp.cos(angles) * norm_scale, -jnp.sin(angles) * norm_scale]).astype(
        jnp.bfloat16
    )


def on_device(samples, fir, chan_assign, input_order):
    own_frames = samples[0]
    frames_quarter, slots_dev, frame_len = own_frames.shape
    taps_count = fir.shape[0]
    chan_count = lax.axis_size("chan")
    group_count = chan_count // QUART
    history_len = taps_count - 1
    lead_len = min(frames_quarter, history_len)
    tail_frames = own_frames[frames_quarter - lead_len :]
    pieces = shifted(tail_frames, "chan", 1 * group_count)
    extended = jnp.concatenate([pieces, own_frames], axis=0)
    dft_table = make_table(chan_assign, frame_len)
    chan_total = chan_assign.shape[0]
    chan_dev = chan_total // chan_count
    inputs_all = input_order.shape[0]
    inverse = jnp.argsort(input_order)
    spectra_total = QUART * frames_quarter
    accum = jnp.zeros((frames_quarter, slots_dev, frame_len), jnp.float32)
    for tap_index in range(taps_count):
        begin = 0 + history_len - tap_index
        accum = accum + fir[tap_index][None, None, :] * extended[
            begin : begin + frames_quarter
        ].astype(jnp.float32)
    filtered = accum.astype(jnp.bfloat16)
    spectra = jnp.einsum("pcn,fin->cfpi", dft_table, filtered, preferred_element_type=jnp.float32)
    spectra = spectra.astype(jnp.bfloat16).reshape(
        chan_count, chan_dev, frames_quarter, 2, slots_dev
    )
    received = lax.all_to_all(spectra, "chan", split_axis=0, concat_axis=4, tiled=True)
    items = received.shape[1]
    row_count = received.shape[2]
    split_parts = received.reshape(items, row_count, 2, QUART, inputs_all)
    ordered = jnp.take(split_parts, inverse, axis=4)
    stacked = ordered.reshape(items, row_count * 2 * QUART, inputs_all)
    real_rows = ordered[:, :, 0].reshape(items, row_count * QUART, inputs_all)
    imag_rows = ordered[:, :, 1].reshape(items, row_count * QUART, inputs_all)
    auto_sum = jnp.einsum("kra,krb->kab", stacked, stacked, preferred_element_type=jnp.float32)
    cross_sum = jnp.einsum("kra,krb->kab", real_rows, imag_rows, preferred_element_type=jnp.float32)
    row_index = lax.broadcasted_iota(jnp.int32, (inputs_all, inputs_all), 0)
    col_index = lax.broadcasted_iota(jnp.int32, (inputs_all, inputs_all), 1)
    upper_mask = (row_index <= col_index)[None, :, :]
    packed = (
        jnp.where(upper_mask, auto_sum, cross_sum - jnp.swapaxes(cross_sum, 1, 2)) / spectra_total
    )
    return packed.astype(jnp.bfloat16)


def solution(mesh):
    in_specs = (P(("grp", "chan"), None, None, None), P(), P(), P())
    out_specs = P(("grp", "chan"), None, None)
    return jax.shard_map(
        on_device, mesh=mesh, in_specs=in_specs, out_specs=out_specs, check_vma=False
    )
```

profile of v0, /device:TPU:13, one launch (start us, length us, event | category | flops | bytes accessed | tf_op | source)
XLA Modules:
  0.0 708.8 jit_solution(15074221744417982181)
XLA Ops:
  0.0 4.2 slice_bitcast_fusion
  4.2 3.2 collective-permute-start
  7.4 1.3 fusion.34
  8.7 5.6 multiply_convert_fusion.1
  14.3 161.9 %collective-permute-done = bf16[15,256,1024]{2,1,0:T(8,128)(2,1)} collective-permute-done((bf16[15,256,1024]{2,1,0:T(8,128)(2,1)S(1)}, bf16[15,256,1024]{2,1,0:T(8,128)(2,1)}, u32[]{:S(2)}, u32[]{:S(2)}) %collective-permute-start) | collective-permute-done | bytes 7864352 | tf_op jit(solution)/shard_map/ppermute | solution.py:14
  176.3 58.6 %fusion.41 = bf16[16,256,1024,1]{2,1,3,0:T(8,128)(2,1)} fusion(bf16[16,256,1024]{2,1,0:T(8,128)(2,1)} %bitcast.64, bf16[15,256,1024]{2,1,0:T(8,128)(2,1)} %collective-permute-done, f32[1024]{0:T(1024)S(1)} %bitcast.80, f32[1024]{0:T(1024)S(1)} %bitcast.81, f32[1024]{0:T(1024)S(1)} %bitcast.67, f32[1024]{0:T(1024)S(1)} %bitcast.68, ...), kind=kLoop, calls=%fused_computation.51.clone.clone.clone.2 | loop fusion | flops 264241152 | bytes 24707072 | tf_op jit(solution)/shard_map/pcn,fin->cfpi/dot_general | solution.py:51
  234.9 8.2 %fusion.20 = bf16[16,256,2,256]{1,3,2,0:T(8,128)(2,1)S(1)} fusion(bf16[1,256,1024]{2,1,0:T(8,128)(2,1)S(1)} %get-tuple-element.26, bf16[1,256,1024]{2,1,0:T(8,128)(2,1)S(1)} %get-tuple-element.25, bf16[16,256,1024,1]{2,1,3,0:T(8,128)(2,1)} %fusion.41), kind=kOutput, calls=%fused_computation.56 | convolution fusion | flops 4299161600 | bytes 13631488 | tf_op jit(solution)/shard_map/pcn,fin->cfpi/dot_general | solution.py:51
  243.1 0.0 copy-start
  243.1 6.5 copy.16
  249.6 7.4 %all-to-all-start = ((bf16[16,16,16,2,256]{4,3,2,1,0:T(2,128)(2,1)}), bf16[16,16,16,2,256]{4,3,2,1,0:T(2,128)(2,1)}, u32[]{:S(2)}, u32[]{:S(2)}) async-start(bf16[16,16,16,2,256]{4,3,2,1,0:T(2,128)(2,1)} %copy.16), calls=%async_computation | async-start | bytes 8388608 | tf_op jit(solution)/shard_map/all_to_all | solution.py:55
  257.0 0.0 copy-done
  257.0 4.4 sort.17
  261.3 0.3 iota_compare_fusion
  261.7 87.7 %all-to-all-done = bf16[16,16,16,2,256]{4,3,2,1,0:T(2,128)(2,1)} async-done(((bf16[16,16,16,2,256]{4,3,2,1,0:T(2,128)(2,1)}), bf16[16,16,16,2,256]{4,3,2,1,0:T(2,128)(2,1)}, u32[]{:S(2)}, u32[]{:S(2)}) %all-to-all-start) | async-done | bytes 4194336 | tf_op jit(solution)/shard_map/all_to_all | solution.py:55
  349.4 32.4 %copy.26 = bf16[1,16,16,2,16,256]{2,1,5,4,3,0:T(8,128)(2,1)} copy(bf16[1,16,16,2,16,256]{5,3,2,1,4,0:T(2,128)(2,1)} %bitcast.24) | data formatting | bytes 8388608 | tf_op jit(solution)/shard_map/reshape | solution.py:58
  381.8 36.7 %gather_fusion = bf16[1024,16,16,2,4]{2,1,4,3,0:T(8,128)(2,1)} fusion(bf16[16,16,2,4,1024]{1,0,4,3,2:T(8,128)(2,1)} %bitcast.63, s32[1024]{0:T(1024)S(1)} %fusion.31), kind=kCustom, calls=%fused_computation | custom fusion | bytes 8392704 | tf_op jit(solution)/shard_map/jit(_take)/gather | solution.py:59
  418.4 35.7 %copy.19 = bf16[16,16,2,4,1024]{4,0,3,2,1:T(8,128)(2,1)} copy(bf16[16,16,2,4,1024]{1,0,3,2,4:T(8,128)(2,1)} %bitcast.62) | data formatting | bytes 8388608 | tf_op jit(solution)/shard_map/jit(_take)/gather | solution.py:59
  454.1 22.7 %broadcast_select_fusion = bf16[16,16,2,4,1024]{1,0,3,2,4:T(8,128)(2,1)} fusion(pred[1024]{0:T(1024)(128)(4,1)S(1)} %compare_and_fusion, bf16[1024,16,16,2,4]{2,1,4,3,0:T(8,128)(2,1)} %gather_fusion), kind=kLoop, calls=%fused_computation.33 | loop fusion | flops 2097152 | bytes 8389632 | tf_op jit(solution)/shard_map/jit(_take)/select_n | solution.py:59
  476.9 4.5 bitcast_select_fusion
  481.3 25.2 %fusion.33 = (bf16[16,16,1,4,1024]{1,0,3,2,4:T(8,128)(2,1)}, bf16[16,16,1,4,1024]{1,0,3,2,4:T(8,128)(2,1)}) fusion(bf16[16,16,2,4,1024]{1,0,3,2,4:T(8,128)(2,1)} %broadcast_select_fusion), kind=kLoop, calls=%fused_computation.75 | loop fusion | bytes 8388608 | tf_op jit(solution)/shard_map/slice | solution.py:62
  506.6 21.9 %copy.23 = bf16[16,16,1,4,1024]{4,3,1,0,2:T(4,128)(2,1)} copy(bf16[16,16,1,4,1024]{1,0,3,2,4:T(8,128)(2,1)} %get-tuple-element.7) | data formatting | bytes 4194304 | tf_op jit(solution)/shard_map/slice | solution.py:62
  528.5 2.5 reshape_squeeze.7
  531.0 21.9 %copy.22 = bf16[16,16,1,4,1024]{4,3,1,0,2:T(4,128)(2,1)} copy(bf16[16,16,1,4,1024]{1,0,3,2,4:T(8,128)(2,1)} %get-tuple-element.8) | data formatting | bytes 4194304 | tf_op jit(solution)/shard_map/slice | solution.py:61
  552.9 4.0 reshape_squeeze.6
  556.9 24.8 %fusion.35 = f32[16,1024,1024]{2,1,0:T(8,128)} fusion(bf16[16,64,1024]{2,1,0:T(8,128)(2,1)} %reshape_squeeze.6, bf16[16,64,1024]{2,1,0:T(8,128)(2,1)S(1)} %reshape_squeeze.7), kind=kOutput, calls=%fused_computation.77 | convolution fusion | flops 2147483648 | bytes 71303168 | tf_op jit(solution)/shard_map/kra,krb->kab/dot_general | solution.py:64
  581.7 62.8 %copy.24 = f32[16,1024,1024]{1,2,0:T(8,128)} copy(f32[16,1024,1024]{2,1,0:T(8,128)} %fusion.35) | data formatting | bytes 134217728 | tf_op jit(solution)/shard_map/kra,krb->kab/dot_general | solution.py:64
  644.5 64.2 %fusion.2 = bf16[16,1024,1024]{2,1,0:T(8,128)(2,1)} fusion(f32[16,1024,1024]{2,1,0:T(8,128)} %fusion.35, f32[16,1024,1024]{1,2,0:T(8,128)} %copy.24, pred[1024,1024]{1,0:T(8,128)(4,1)S(1)} %iota_compare_fusion, bf16[16,128,1024]{2,0,1:T(8,128)(2,1)} %bitcast_select_fusion), kind=kOutput, calls=%fused_computation.4 | convolution fusion | flops 4362076160 | bytes 173015040 | tf_op jit(solution)/shard_map/kra,krb->kab/dot_general | solution.py:63
  (3 shorter events, 0.0 us)
Async XLA Ops:
  4.2 172.1 %collective-permute-start = (bf16[15,256,1024]{2,1,0:T(8,128)(2,1)S(1)}, bf16[15,256,1024]{2,1,0:T(8,128)(2,1)}, u32[]{:S(2)}, u32[]{:S(2)}) collective-permute-start(bf16[15,256,1024]{2,1,0:T(8,128)(2,1)S(1)} %slice_bitcast_fusion), channel_id=1, source_target_pairs={{0,4},{1,5},{2,6},{3,7},{4,8},{5,9},{6,10},{7,11},{8,12},{9,13},{1... | collective-permute-start | bytes 23592968 | tf_op jit(solution)/shard_map/ppermute | solution.py:14
  243.1 13.9 %copy-start = (s32[1024]{0:T(1024)S(1)}, s32[1024]{0:T(1024)}, u32[]{:S(2)}) copy-start(s32[1024]{0:T(1024)} %param.7) | copy-start | bytes 12292
  249.6 99.8 %all-to-all-start = ((bf16[16,16,16,2,256]{4,3,2,1,0:T(2,128)(2,1)}), bf16[16,16,16,2,256]{4,3,2,1,0:T(2,128)(2,1)}, u32[]{:S(2)}, u32[]{:S(2)}) async-start(bf16[16,16,16,2,256]{4,3,2,1,0:T(2,128)(2,1)} %copy.16), calls=%async_computation | async-start | bytes 8388608 | tf_op jit(solution)/shard_map/all_to_all | solution.py:55
where the time goes:
time: 714 us; the launch traced here: 709 us
  local copies, waits for them, and re-layouts  255 us (36%)
  waiting for transfers between devices  250 us (35%)
  matrix products  97.2 us (14%)
  other arithmetic  96.2 us (13%)
  starting transfers between devices  10.6 us (1%)
    ppermute x1, waiting for transfers between devices, shifted(): lax.ppermute(value, axis, [(source, source + steps) for source in range(i...  162 us
    all_to_all x1, waiting for transfers between devices, on_device(): lax.all_to_all(spectra, 'chan', split_axis=0, concat_axis=4, tiled=True)  87.7 us
    gather x2, local copies, waits for them, and re-layouts, on_device(): ordered = jnp.take(split_parts, inverse, axis=4)  72.4 us
    dot_general x1, matrix products, on_device(): jnp.einsum('kra,krb->kab', stacked, stacked, preferred_element_type=jnp.f...  64.2 us
    dot_general x1, local copies, waits for them, and re-layouts, on_device(): jnp.einsum('kra,krb->kab', real_rows, imag_rows, preferred_element_type=j...  62.8 us
    dot_general x1, other arithmetic, on_device(): jnp.einsum('pcn,fin->cfpi', dft_table, filtered, preferred_element_type=j...  58.6 us
    slice x2, local copies, waits for them, and re-layouts, on_device(): imag_rows = ordered[:, :, 1].reshape(items, row_count * QUART, inputs_all)  47.1 us
    reshape x1, local copies, waits for them, and re-layouts, on_device(): split_parts = received.reshape(items, row_count, 2, QUART, inputs_all)  32.4 us
  transfers between devices with their start and end apart: 2, of which 2 were waited for; matrix products, arithmetic and copies ran while one was open for 2% of the time, Pallas kernels for 0%

commit v1 on v0

v1 whole, which is shorter than its diff:
```python
import functools
import math

import jax
import jax.numpy as jnp
from jax import lax
from jax.experimental import pallas as pl
from jax.experimental.pallas import tpu as pltpu
from jax.sharding import PartitionSpec as P

QUART = 4
LANES = 128


def make_table(chans, frame_len):
    samples_index = jnp.arange(frame_len, dtype=jnp.int32)
    phase_index = chans[:, None] * samples_index[None, :] % frame_len
    angles = phase_index.astype(jnp.float32) * (2.0 * math.pi / frame_len)
    norm_scale = 1.0 / math.sqrt(frame_len)
    table = jnp.stack([jnp.cos(angles) * norm_scale, -jnp.sin(angles) * norm_scale], axis=1)
    return table.astype(jnp.bfloat16).reshape(-1, frame_len)


def front_kernel(sets, x_ref, fir_ref, table_ref, *rest):
    outs, (filt, spread) = rest[: 2 * sets], rest[2 * sets :]
    frames, slots, lanes = x_ref.shape
    taps = fir_ref.shape[0]
    step = pl.program_id(0)
    columns = pl.ds(pl.multiple_of(step * lanes, lanes), lanes)

    def filter_rows(block, carry):
        rows = pl.ds(pl.multiple_of(block * 16, 16), 16)
        own = [x_ref[f, rows, :].astype(jnp.float32) for f in range(frames)]
        for out in range(2 * frames):
            total = None
            for source in range(max(0, out - taps + 1), min(frames, out + 1)):
                term = own[source] * fir_ref[out - source : out - source + 1, :]
                total = term if total is None else total + term
            if total is None:
                total = jnp.zeros((16, lanes), jnp.float32)
            filt[out, rows, columns] = total.astype(jnp.bfloat16)
        return carry

    lax.fori_loop(0, slots // 16, filter_rows, 0)

    @pl.when(step == pl.num_programs(0) - 1)
    def _():
        table_rows = table_ref.shape[0] // sets
        pair = 2 if slots % LANES == 0 else 1
        for part in range(2):
            for each in range(sets):
                table = table_ref[each * table_rows : (each + 1) * table_rows, :]

                def transform(index, carry):
                    frame = index * pair
                    block = filt[pl.ds(part * frames + frame, pair)]
                    result = lax.dot_general(
                        table,
                        block.reshape(pair * slots, -1),
                        (((1,), (1,)), ((), ())),
                        preferred_element_type=jnp.float32,
                    )
                    for one in range(pair):
                        spread[pl.ds(frame + one, table_rows, stride=frames), :] = result[
                            :, one * slots : (one + 1) * slots
                        ]
                    return carry

                lax.fori_loop(0, frames // pair, transform, 0)
                outs[part * sets + each][...] = spread[...].astype(jnp.bfloat16)


def front(x, fir, table, block, blocks, sets):
    frames, slots_dev, frame_len = x.shape
    slots = slots_dev // blocks
    table_rows = table.shape[0]
    out_rows = table_rows // sets * frames
    return pl.pallas_call(
        functools.partial(front_kernel, sets),
        grid=(frame_len // LANES,),
        in_specs=[
            pl.BlockSpec((frames, slots, LANES), lambda j: (0, block, j)),
            pl.BlockSpec((fir.shape[0], LANES), lambda j: (0, j)),
            pl.BlockSpec((table_rows, frame_len), lambda j: (0, 0), pipeline_mode=pl.Buffered(1)),
        ],
        out_specs=[pl.BlockSpec((out_rows, slots), lambda j: (0, 0), pipeline_mode=pl.Buffered(1))]
        * (2 * sets),
        out_shape=[jax.ShapeDtypeStruct((out_rows, slots), jnp.bfloat16)] * (2 * sets),
        scratch_shapes=[
            pltpu.VMEM((2 * frames, slots, frame_len), jnp.bfloat16),
            pltpu.VMEM((out_rows, slots), jnp.float32),
        ],
        cost_estimate=pl.CostEstimate(
            flops=4 * frames * slots * frame_len * table_rows,
            bytes_accessed=2 * frames * slots * frame_len + 4 * table_rows * frames * slots,
            transcendentals=0,
        ),
        name="front",
    )(x, fir, table)


def back_kernel(blocks, groups, scale, *refs):
    order_ref, datas = refs[0], refs[1 : 1 + blocks]
    out_ref, pick, ordered = refs[-3], refs[-2], refs[-1]
    inputs = out_ref.shape[-1]
    tile = min(256, inputs)

    @pl.when(pl.program_id(0) == 0)
    def _():
        for first in range(0, inputs, tile):
            wanted = first + lax.broadcasted_iota(jnp.int32, (tile, inputs), 0)
            hit = jnp.where(order_ref[...] == wanted, 1.0, 0.0)
            pick[first : first + tile, :] = hit.astype(jnp.bfloat16)

    pieces = []
    for group in range(groups):
        for data in datas:
            planes = data.shape[1] // 2
            real, imag = [], []
            for quarter in range(QUART):
                source = quarter * groups + group
                real.append(data[source, :planes, :])
                imag.append(data[source, planes:, :])
            rows = []
            for quarter in range(QUART):
                rows += [real[quarter], imag[quarter]]
            for quarter in range(QUART):
                rows += [imag[quarter], -real[quarter]]
            pieces.append(jnp.concatenate(rows, axis=0))
    stacked = jnp.concatenate(pieces, axis=1)
    depth = stacked.shape[0] // 2
    contract = (((1,), (1,)), ((), ()))
    for first in range(0, inputs, tile):
        part = pl.ds(first, tile)
        ordered[part, :] = lax.dot_general(
            pick[part, :], stacked, contract, preferred_element_type=jnp.float32
        ).astype(jnp.bfloat16)
    for first in range(0, inputs, tile):
        left = ordered[first : first + tile, :depth]
        for other in range(0, inputs, tile):
            place = pl.ds(other, tile)
            if other >= first:
                upper = lax.dot_general(
                    left, ordered[place, :depth], contract, preferred_element_type=jnp.float32
                )
            if other <= first:
                lower = lax.dot_general(
                    left, ordered[place, depth:], contract, preferred_element_type=jnp.float32
                )
            if other > first:
                result = upper
            elif other < first:
                result = lower
            else:
                row = lax.broadcasted_iota(jnp.int32, (tile, tile), 0)
                column = lax.broadcasted_iota(jnp.int32, (tile, tile), 1)
                result = jnp.where(row <= column, upper, lower)
            out_ref[0, first : first + tile, place] = (result * scale).astype(jnp.bfloat16)


def back(order, datas, each, sets, chan_dev, earlier):
    sources, rows, slots = datas[0].shape
    inputs = order.shape[1]
    groups = sources // QUART
    held = chan_dev // sets
    per_chan = rows // held
    spectra_total = QUART * (per_chan // 2)
    operands = [order] + list(datas)
    in_specs = [pl.BlockSpec((1, inputs), lambda k: (0, 0))]
    in_specs += [pl.BlockSpec((sources, per_chan, slots), lambda k: (0, k, 0))] * len(datas)
    aliases = {}
    kernel = functools.partial(back_kernel, len(datas), groups, 1.0 / spectra_total)
    if earlier is not None:
        aliases = {len(operands): 0}
        operands.append(earlier)
        in_specs.append(pl.BlockSpec(memory_space=pl.ANY))
    return pl.pallas_call(
        kernel,
        grid=(held,),
        in_specs=in_specs,
        out_specs=pl.BlockSpec((1, inputs, inputs), lambda k: (k + each * held, 0, 0)),
        out_shape=jax.ShapeDtypeStruct((chan_dev, inputs, inputs), jnp.bfloat16),
        scratch_shapes=[
            pltpu.VMEM((inputs, inputs), jnp.bfloat16),
            pltpu.VMEM((inputs, 4 * QUART * (per_chan // 2)), jnp.bfloat16),
        ],
        input_output_aliases=aliases,
        cost_estimate=pl.CostEstimate(
            flops=held * inputs * inputs * 1024,
            bytes_accessed=2 * held * inputs * inputs,
            transcendentals=0,
        ),
        name="back",
    )(*operands)


def on_device(samples, fir, chan_assign, input_order):
    own_frames = samples[0]
    frames, slots_dev, frame_len = own_frames.shape
    chan_count = lax.axis_size("chan")
    group_count = chan_count // QUART
    chan_dev = chan_assign.shape[0] // chan_count
    sets = 2 if chan_dev % 2 == 0 else 1
    held = chan_dev // sets
    blocks = 2 if slots_dev % (2 * LANES) == 0 else 1
    chans = chan_assign.reshape(chan_count, sets, held).transpose(1, 0, 2).reshape(-1)
    table = make_table(chans, frame_len)
    order = input_order[None, :]
    per_dest = held * 2 * frames

    ready = [[None] * blocks for _ in range(sets)]
    for block in range(blocks):
        parts = front(own_frames, fir, table, block, blocks, sets)
        for each in range(sets):
            both = jnp.concatenate(
                [
                    parts[part * sets + each].reshape(chan_count, per_dest, -1)
                    for part in range(2)
                ],
                axis=1,
            )
            got = lax.all_to_all(both, "chan", split_axis=0, concat_axis=0, tiled=True)
            own = got[:, :per_dest].astype(jnp.float32)
            late = got[: chan_count - group_count, per_dest:].astype(jnp.float32)
            late = jnp.pad(late, ((group_count, 0), (0, 0), (0, 0)))
            ready[each][block] = (own + late).astype(jnp.bfloat16)
    vis = None
    for each in range(sets):
        vis = back(order, ready[each], each, sets, chan_dev, vis)
    return vis


def solution(mesh):
    in_specs = (P(("grp", "chan"), None, None, None), P(), P(), P())
    out_specs = P(("grp", "chan"), None, None)
    return jax.shard_map(
        on_device, mesh=mesh, in_specs=in_specs, out_specs=out_specs, check_vma=False
    )
```

time: 714 us -> 267 us (0.37)
  local copies, waits for them, and re-layouts: 255 us -> 6.79 us
  waiting for transfers between devices: 250 us -> 132 us
  matrix products: 97.2 us -> 0 us
  Pallas kernels: 0 us -> 81.6 us
  other arithmetic: 96.2 us -> 25.2 us
  starting transfers between devices: 10.6 us -> 21 us
    ppermute x1 -> x0, waiting for transfers between devices: 162 us -> none  [shifted(): lax.ppermute(value, axis, [(source, source + steps) for source in range(i...]
    dot_general x3 -> x0, matrix products: 97.2 us -> none  [the longest x1 64.2 us: on_device(): jnp.einsum('kra,krb->kab', stacked, stacked, preferred_element_type=jnp.f...]
    pallas_call x0 -> x4, Pallas kernels: none -> 81.6 us  [the longest x2 51.6 us: front(): pl.pallas_call(functools.partial(front_kernel, sets), grid=(frame_len //...]
    gather x2 -> x0, local copies, waits for them, and re-layouts: 72.4 us -> none  [on_device(): ordered = jnp.take(split_parts, inverse, axis=4)]
    slice x5 -> x4, local copies, waits for them, and re-layouts: 74.5 us -> 3.62 us  [on_device(): late = got[:chan_count - group_count, per_dest:].astype(jnp.float32)]
    dot_general x1 -> x0, local copies, waits for them, and re-layouts: 62.8 us -> none  [on_device(): jnp.einsum('kra,krb->kab', real_rows, imag_rows, preferred_element_type=j...]
    dot_general x1 -> x0, other arithmetic: 58.6 us -> none  [on_device(): jnp.einsum('pcn,fin->cfpi', dft_table, filtered, preferred_element_type=j...]
    all_to_all x1 -> x4, waiting for transfers between devices: 87.7 us -> 132 us  [on_device(): got = lax.all_to_all(both, 'chan', split_axis=0, concat_axis=0, tiled=True)]
  transfers between devices with their start and end apart: 2 -> 4, of which waited for: 2 -> 4; matrix products, arithmetic and copies ran while one was open for 2% -> 6% of each run, Pallas kernels for 0% -> 15%
where the time goes in v1:
time: 267 us
  waiting for transfers between devices  132 us (49%)
  Pallas kernels  81.6 us (31%)
  other arithmetic  25.2 us (9%)
  starting transfers between devices  21 us (8%)
  local copies, waits for them, and re-layouts  6.79 us (3%)
    all_to_all x4, waiting for transfers between devices, on_device(): got = lax.all_to_all(both, 'chan', split_axis=0, concat_axis=0, tiled=True)  132 us
    pallas_call x2, Pallas kernels, front(): pl.pallas_call(functools.partial(front_kernel, sets), grid=(frame_len //...  51.6 us
    pallas_call x2, Pallas kernels, back(): pl.pallas_call(kernel, grid=(held,), in_specs=in_specs, out_specs=pl.Bloc...  29.9 us
    all_to_all x4, starting transfers between devices, on_device(): got = lax.all_to_all(both, 'chan', split_axis=0, concat_axis=0, tiled=True)  21 us
    concatenate x4, other arithmetic, on_device(): jnp.concatenate([parts[part * sets + each].reshape(chan_count, per_dest,...  11.6 us
    convert_element_type x4, other arithmetic, on_device(): ready[each][block] = (own + late).astype(jnp.bfloat16)  8.62 us
  transfers between devices with their start and end apart: 4, of which 4 were waited for; matrix products, arithmetic and copies ran while one was open for 6% of the time, Pallas kernels for 15%

profile of v1, /device:TPU:13, one launch (start us, length us, event | category | flops | bytes accessed | tf_op | source)
XLA Modules:
  0.0 266.6 jit_solution(11640115229016038409)
XLA Ops:
  0.0 0.8 reshape.153
  0.8 0.1 mul.63
  0.9 4.9 %multiply_convert_fusion.1 = (bf16[256,1,1024]{2,0,1:T(8,128)(2,1)S(1)}, bf16[256,1,1024]{2,0,1:T(8,128)(2,1)S(1)}) fusion(s32[256]{0:T(256)S(1)} %mul.63), kind=kLoop, calls=%fused_computation.16 | loop fusion | flops 4980736 | bytes 1049600 | tf_op jit(solution)/shard_map/convert.8
  5.8 0.1 pad_maximum_fusion.4
  5.9 1.1 copy.8
  7.0 1.2 convert_element_type.53.table_ref
  8.2 25.8 %front.3 = (bf16[4096,128]{1,0:T(8,128)(2,1)}, bf16[4096,128]{1,0:T(8,128)(2,1)}, bf16[4096,128]{1,0:T(8,128)(2,1)}, bf16[4096,128]{1,0:T(8,128)(2,1)}) custom-call(bf16[16,256,1024]{2,1,0:T(8,128)(2,1)} %bitcast.22, f32[16,1024]{1,0:T(8,128)} %fir_ref.3, bf16[512,1024]{1,0:T(8,128)(2,1)} %convert_element_type.53.table_ref), custom_call_target="tpu_custom_call" | custom-call | flops 4294967296 | bytes 8388608 | tf_op jit(solution)/shard_map/front/pallas_call | solution.py:78
  34.0 3.1 %pad_maximum_fusion.1 = bf16[16,512,128]{2,1,0:T(8,128)(2,1)} fusion(bf16[16,256,128]{2,1,0:T(8,128)(2,1)} %bitcast.18, bf16[16,256,128]{2,1,0:T(8,128)(2,1)} %bitcast.17), kind=kLoop, calls=%fused_computation.1 | loop fusion | flops 4194304 | bytes 4194304 | tf_op jit(solution)/shard_map/concatenate | solution.py:215
  37.0 0.0 copy-start.1
  37.0 6.7 %all-to-all-start.1 = ((bf16[16,512,128]{2,1,0:T(8,128)(2,1)}), bf16[16,512,128]{2,1,0:T(8,128)(2,1)S(1)}, u32[]{:S(2)}, u32[]{:S(2)}) async-start(bf16[16,512,128]{2,1,0:T(8,128)(2,1)} %pad_maximum_fusion.1), calls=%async_computation.1 | async-start | bytes 4194304 | tf_op jit(solution)/shard_map/all_to_all | solution.py:222
  43.7 0.0 copy-done.1
  43.7 2.7 %pad_maximum_fusion.3 = bf16[16,512,128]{2,1,0:T(8,128)(2,1)} fusion(bf16[16,256,128]{2,1,0:T(8,128)(2,1)} %bitcast.14, bf16[16,256,128]{2,1,0:T(8,128)(2,1)S(1)} %bitcast.13), kind=kLoop, calls=%fused_computation.3 | loop fusion | flops 4194304 | bytes 4194304 | tf_op jit(solution)/shard_map/concatenate | solution.py:215
  46.4 44.7 %all-to-all-done.1 = bf16[16,512,128]{2,1,0:T(8,128)(2,1)S(1)} async-done(((bf16[16,512,128]{2,1,0:T(8,128)(2,1)}), bf16[16,512,128]{2,1,0:T(8,128)(2,1)S(1)}, u32[]{:S(2)}, u32[]{:S(2)}) %all-to-all-start.1) | async-done | bytes 2097184 | tf_op jit(solution)/shard_map/all_to_all | solution.py:222
  91.1 4.8 %all-to-all-start.3 = ((bf16[16,512,128]{2,1,0:T(8,128)(2,1)}), bf16[16,512,128]{2,1,0:T(8,128)(2,1)}, u32[]{:S(2)}, u32[]{:S(2)}) async-start(bf16[16,512,128]{2,1,0:T(8,128)(2,1)} %pad_maximum_fusion.3), calls=%async_computation.3 | async-start | bytes 4194304 | tf_op jit(solution)/shard_map/all_to_all | solution.py:222
  95.9 25.9 %front.2 = (bf16[4096,128]{1,0:T(8,128)(2,1)}, bf16[4096,128]{1,0:T(8,128)(2,1)}, bf16[4096,128]{1,0:T(8,128)(2,1)}, bf16[4096,128]{1,0:T(8,128)(2,1)}) custom-call(bf16[16,256,1024]{2,1,0:T(8,128)(2,1)} %bitcast.23, f32[16,1024]{1,0:T(8,128)} %fir_ref.3, bf16[512,1024]{1,0:T(8,128)(2,1)} %convert_element_type.53.table_ref), custom_call_target="tpu_custom_call" | custom-call | flops 4294967296 | bytes 8388608 | tf_op jit(solution)/shard_map/front/pallas_call | solution.py:78
  121.8 3.1 %pad_maximum_fusion.2 = bf16[16,512,128]{2,1,0:T(8,128)(2,1)} fusion(bf16[16,256,128]{2,1,0:T(8,128)(2,1)} %bitcast.16, bf16[16,256,128]{2,1,0:T(8,128)(2,1)} %bitcast.15), kind=kLoop, calls=%fused_computation.2 | loop fusion | flops 4194304 | bytes 4194304 | tf_op jit(solution)/shard_map/concatenate | solution.py:215
  124.8 0.0 copy-start
  124.8 18.6 %all-to-all-done.3 = bf16[16,512,128]{2,1,0:T(8,128)(2,1)} async-done(((bf16[16,512,128]{2,1,0:T(8,128)(2,1)}), bf16[16,512,128]{2,1,0:T(8,128)(2,1)}, u32[]{:S(2)}, u32[]{:S(2)}) %all-to-all-start.3) | async-done | bytes 2097184 | tf_op jit(solution)/shard_map/all_to_all | solution.py:222
  143.4 4.8 %all-to-all-start.2 = ((bf16[16,512,128]{2,1,0:T(8,128)(2,1)}), bf16[16,512,128]{2,1,0:T(8,128)(2,1)}, u32[]{:S(2)}, u32[]{:S(2)}) async-start(bf16[16,512,128]{2,1,0:T(8,128)(2,1)} %pad_maximum_fusion.2), calls=%async_computation.2 | async-start | bytes 4194304 | tf_op jit(solution)/shard_map/all_to_all | solution.py:222
  148.2 0.0 copy-done
  148.2 2.7 %pad_maximum_fusion = bf16[16,512,128]{2,1,0:T(8,128)(2,1)} fusion(bf16[16,256,128]{2,1,0:T(8,128)(2,1)} %bitcast.12, bf16[16,256,128]{2,1,0:T(8,128)(2,1)S(1)} %bitcast.11), kind=kLoop, calls=%fused_computation | loop fusion | flops 4194304 | bytes 4194304 | tf_op jit(solution)/shard_map/concatenate | solution.py:215
  150.9 44.8 %all-to-all-done.2 = bf16[16,512,128]{2,1,0:T(8,128)(2,1)} async-done(((bf16[16,512,128]{2,1,0:T(8,128)(2,1)}), bf16[16,512,128]{2,1,0:T(8,128)(2,1)}, u32[]{:S(2)}, u32[]{:S(2)}) %all-to-all-start.2) | async-done | bytes 2097184 | tf_op jit(solution)/shard_map/all_to_all | solution.py:222
  195.7 4.8 %all-to-all-start = ((bf16[16,512,128]{2,1,0:T(8,128)(2,1)}), bf16[16,512,128]{2,1,0:T(8,128)(2,1)}, u32[]{:S(2)}, u32[]{:S(2)}) async-start(bf16[16,512,128]{2,1,0:T(8,128)(2,1)} %pad_maximum_fusion), calls=%async_computation | async-start | bytes 4194304 | tf_op jit(solution)/shard_map/all_to_all | solution.py:222
  200.5 0.1 slice.35
  200.6 1.2 slice.39
  201.8 1.2 slice.37
  202.9 1.3 add_convert_fusion.2.refs_2_
  204.2 2.4 add_convert_fusion.refs_2_
  206.7 2.4 add_convert_fusion.1.refs_1_
  209.1 14.9 %back.2.refs_3_ = bf16[16,1024,1024]{2,1,0:T(8,128)(2,1)} custom-call(s32[1,1024]{1,0:T(1,128)} %bitcast.20, bf16[16,256,128]{2,1,0:T(8,128)(2,1)} %add_convert_fusion.1.refs_1_, bf16[16,256,128]{2,1,0:T(8,128)(2,1)} %add_convert_fusion.refs_2_), custom_call_target="tpu_custom_call" | custom-call | flops 8589934592 | bytes 16777216 | tf_op jit(solution)/shard_map/back/pallas_call | solution.py:177
  224.1 23.9 %all-to-all-done = bf16[16,512,128]{2,1,0:T(8,128)(2,1)} async-done(((bf16[16,512,128]{2,1,0:T(8,128)(2,1)}), bf16[16,512,128]{2,1,0:T(8,128)(2,1)}, u32[]{:S(2)}, u32[]{:S(2)}) %all-to-all-start) | async-done | bytes 2097184 | tf_op jit(solution)/shard_map/all_to_all | solution.py:222
  248.0 1.2 slice.33
  249.2 2.4 add_convert_fusion.3.refs_1_
  251.7 15.0 %back.3 = bf16[16,1024,1024]{2,1,0:T(8,128)(2,1)} custom-call(s32[1,1024]{1,0:T(1,128)} %bitcast.21, bf16[16,256,128]{2,1,0:T(8,128)(2,1)} %add_convert_fusion.3.refs_1_, bf16[16,256,128]{2,1,0:T(8,128)(2,1)} %add_convert_fusion.2.refs_2_, bf16[16,1024,1024]{2,1,0:T(8,128)(2,1)} %back.2.refs_3_), custom_call_target="tpu_custom_call", output_to_operand_aliasing={{}: (3, {})} | custom-call | flops 8589934592 | bytes 16777216 | tf_op jit(solution)/shard_map/back/pallas_call | solution.py:177
  (1 shorter events, 0.0 us)
Async XLA Ops:
  37.0 6.7 %copy-start.1 = (bf16[4096,128]{1,0:T(8,128)(2,1)S(1)}, bf16[4096,128]{1,0:T(8,128)(2,1)}, u32[]{:S(2)}) copy-start(bf16[4096,128]{1,0:T(8,128)(2,1)} %get-tuple-element.19) | copy-start | bytes 3145732
  37.0 54.1 %all-to-all-start.1 = ((bf16[16,512,128]{2,1,0:T(8,128)(2,1)}), bf16[16,512,128]{2,1,0:T(8,128)(2,1)S(1)}, u32[]{:S(2)}, u32[]{:S(2)}) async-start(bf16[16,512,128]{2,1,0:T(8,128)(2,1)} %pad_maximum_fusion.1), calls=%async_computation.1 | async-start | bytes 4194304 | tf_op jit(solution)/shard_map/all_to_all | solution.py:222
  91.1 52.3 %all-to-all-start.3 = ((bf16[16,512,128]{2,1,0:T(8,128)(2,1)}), bf16[16,512,128]{2,1,0:T(8,128)(2,1)}, u32[]{:S(2)}, u32[]{:S(2)}) async-start(bf16[16,512,128]{2,1,0:T(8,128)(2,1)} %pad_maximum_fusion.3), calls=%async_computation.3 | async-start | bytes 4194304 | tf_op jit(solution)/shard_map/all_to_all | solution.py:222
  124.8 23.4 %copy-start = (bf16[4096,128]{1,0:T(8,128)(2,1)S(1)}, bf16[4096,128]{1,0:T(8,128)(2,1)}, u32[]{:S(2)}) copy-start(bf16[4096,128]{1,0:T(8,128)(2,1)} %get-tuple-element.13) | copy-start | bytes 3145732
  143.4 52.3 %all-to-all-start.2 = ((bf16[16,512,128]{2,1,0:T(8,128)(2,1)}), bf16[16,512,128]{2,1,0:T(8,128)(2,1)}, u32[]{:S(2)}, u32[]{:S(2)}) async-start(bf16[16,512,128]{2,1,0:T(8,128)(2,1)} %pad_maximum_fusion.2), calls=%async_computation.2 | async-start | bytes 4194304 | tf_op jit(solution)/shard_map/all_to_all | solution.py:222
  195.7 52.3 %all-to-all-start = ((bf16[16,512,128]{2,1,0:T(8,128)(2,1)}), bf16[16,512,128]{2,1,0:T(8,128)(2,1)}, u32[]{:S(2)}, u32[]{:S(2)}) async-start(bf16[16,512,128]{2,1,0:T(8,128)(2,1)} %pad_maximum_fusion), calls=%async_computation | async-start | bytes 4194304 | tf_op jit(solution)/shard_map/all_to_all | solution.py:222

commit v2 on v1

v2 whole, which is shorter than its diff:
```python
import functools
import math

import jax
import jax.numpy as jnp
from jax import lax
from jax.experimental import pallas as pl
from jax.experimental.pallas import tpu as pltpu
from jax.sharding import PartitionSpec as P

QUART = 4
LANES = 128


def split_table(chans, frame_len):
    norm_scale = 1.0 / math.sqrt(frame_len)

    def angles(samples):
        phase_index = chans[:, None] * samples[None, :] % frame_len
        return phase_index.astype(jnp.float32) * (2.0 * math.pi / frame_len)

    fine = angles(jnp.arange(LANES, dtype=jnp.int32))
    coarse = angles(jnp.arange(0, frame_len, LANES, dtype=jnp.int32)).T[:, :, None]
    fine = jnp.stack([jnp.cos(fine) * norm_scale, jnp.sin(fine) * norm_scale])
    return fine, jnp.stack([jnp.cos(coarse), jnp.sin(coarse)], axis=1)


def tap_leaves(taps):
    if len(taps) <= 4:
        return [taps]
    low, high = taps[: len(taps) // 2], taps[len(taps) // 2 :]
    middle = [one + other for one, other in zip(low, high)]
    return tap_leaves(low) + tap_leaves(high) + tap_leaves(middle)


def direct(values, taps):
    outs = []
    for out in range(len(values) + len(taps) - 1):
        total = None
        for source in range(max(0, out - len(taps) + 1), min(len(values), out + 1)):
            term = values[source] * taps[out - source]
            total = term if total is None else total + term
        outs.append(total)
    return outs


def product(values, leaves):
    count = len(values)
    if count <= 4:
        return direct(values, next(leaves))
    half = count // 2
    low = product(values[:half], leaves)
    high = product(values[half:], leaves)
    middle = product([one + other for one, other in zip(values[:half], values[half:])], leaves)
    middle = [whole - (one + other) for whole, one, other in zip(middle, low, high)]
    outs = low[:half]
    outs += [low[half + i] + middle[i] for i in range(half - 1)]
    outs += [middle[half - 1]]
    outs += [middle[half + i] + high[i] for i in range(half - 1)]
    return outs + high[half - 1 :]


def front_kernel(sets, x_ref, fir_ref, fine_ref, coarse_ref, *rest):
    outs, (filt, spread, table, coeffs) = rest[:sets], rest[sets:]
    frames, slots, lanes = x_ref.shape
    taps = fir_ref.shape[0]
    step = pl.program_id(0)
    columns = pl.ds(pl.multiple_of(step * lanes, lanes), lanes)
    recursive = taps == frames and frames & (frames - 1) == 0

    chans = fine_ref.shape[1]
    turn = [coarse_ref[0, part] for part in range(2)]
    held = chans // sets
    rows = [fine_ref[0] * turn[0] - fine_ref[1] * turn[1]]
    rows += [-(fine_ref[1] * turn[0] + fine_ref[0] * turn[1])]
    for each in range(sets):
        for part in range(2):
            first = (each * 2 + part) * held
            piece = rows[part][each * held : (each + 1) * held]
            table[first : first + held, columns] = piece.astype(jnp.bfloat16)

    leaves = [fir_ref[tap : tap + 1, :] for tap in range(taps)]
    leaves = tap_leaves(leaves) if recursive else [leaves]
    sizes = [len(leaf) for leaf in leaves]
    for index, row in enumerate(sum(leaves, [])):
        coeffs[index : index + 1, :] = row

    def filter_rows(block, carry):
        rows = pl.ds(pl.multiple_of(block * 16, 16), 16)
        own = [x_ref[f, rows, :].astype(jnp.float32) for f in range(frames)]
        done = []
        for half in range(2):
            values = [one[half * 8 : half * 8 + 8] for one in own]
            starts = [sum(sizes[:i]) for i in range(len(sizes))]
            lists = [
                [coeffs[start + i : start + i + 1, :] for i in range(size)]
                for start, size in zip(starts, sizes)
            ]
            results = product(values, iter(lists)) if recursive else direct(values, lists[0])
            done.append(results)
        for out in range(2 * frames):
            if out < len(done[0]):
                total = jnp.concatenate([done[0][out], done[1][out]], axis=0)
            else:
                total = jnp.zeros((16, lanes), jnp.float32)
            filt[out, rows, columns] = total.astype(jnp.bfloat16)
        return carry

    lax.fori_loop(0, slots // 16, filter_rows, 0)

    @pl.when(step == pl.num_programs(0) - 1)
    def _():
        pair = 2 if slots % LANES == 0 else 1
        for part in range(2):

            def transform(index, carry):
                frame = index * pair
                block = filt[pl.ds(part * frames + frame, pair)]
                result = lax.dot_general(
                    table[...],
                    block.reshape(pair * slots, -1),
                    (((1,), (1,)), ((), ())),
                    preferred_element_type=jnp.float32,
                )
                for one in range(pair):
                    for piece in range(2 * sets):
                        each, which = divmod(piece, 2)
                        start = each * held * 2 * frames + which * frames
                        spread[pl.ds(start + frame + one, held, stride=2 * frames), :] = result[
                            piece * held : (piece + 1) * held, one * slots : (one + 1) * slots
                        ]
                return carry

            lax.fori_loop(0, frames // pair, transform, 0)
            for each in range(sets):
                dests, both_rows, _ = outs[each].shape
                per_dest = both_rows // 2
                block = spread[each * dests * per_dest : (each + 1) * dests * per_dest, :]
                outs[each][:, part * per_dest : (part + 1) * per_dest, :] = block.reshape(
                    dests, per_dest, slots
                ).astype(jnp.bfloat16)


def front(x, fir, fine, coarse, block, blocks, sets, dests):
    frames, slots_dev, frame_len = x.shape
    slots = slots_dev // blocks
    taps = fir.shape[0]
    chans = fine.shape[1]
    out_shape = (dests, chans // sets // dests * 4 * frames, slots)
    return pl.pallas_call(
        functools.partial(front_kernel, sets),
        grid=(frame_len // LANES,),
        in_specs=[
            pl.BlockSpec((frames, slots, LANES), lambda j: (0, block, j)),
            pl.BlockSpec((taps, LANES), lambda j: (0, j)),
            pl.BlockSpec(fine.shape, lambda j: (0, 0, 0), pipeline_mode=pl.Buffered(1)),
            pl.BlockSpec((1, 2, chans, 1), lambda j: (j, 0, 0, 0)),
        ],
        out_specs=[pl.BlockSpec(out_shape, lambda j: (0, 0, 0), pipeline_mode=pl.Buffered(1))]
        * sets,
        out_shape=[jax.ShapeDtypeStruct(out_shape, jnp.bfloat16)] * sets,
        scratch_shapes=[
            pltpu.VMEM((2 * frames, slots, frame_len), jnp.bfloat16),
            pltpu.VMEM((2 * chans * frames, slots), jnp.float32),
            pltpu.VMEM((2 * chans, frame_len), jnp.bfloat16),
            pltpu.VMEM((4 * taps, LANES), jnp.float32),
        ],
        cost_estimate=pl.CostEstimate(
            flops=8 * frames * slots * frame_len * chans,
            bytes_accessed=2 * frames * slots * frame_len + 8 * chans * frames * slots,
            transcendentals=0,
        ),
        name="front",
    )(x, fir, fine, coarse)


def back_kernel(blocks, groups, pair, scale, *refs):
    order_ref, owns, lates = refs[0], refs[1 : 1 + blocks], refs[1 + blocks : 1 + 2 * blocks]
    out_ref, pick, ordered, turned = refs[-4:]
    inputs = out_ref.shape[-1]
    tile = min(256, inputs)

    @pl.when(pl.program_id(0) == 0)
    def _():
        for first in range(0, inputs, tile):
            wanted = first + lax.broadcasted_iota(jnp.int32, (tile, inputs), 0)
            hit = jnp.where(order_ref[...] == wanted, 1.0, 0.0)
            pick[first : first + tile, :] = hit.astype(jnp.bfloat16)

    per_chan = owns[0].shape[1] // pair
    frames = per_chan // 2
    pieces = []
    for group in range(groups):
        for own, late in zip(owns, lates):
            rows = []
            for chan in range(pair):
                for part in range(2):
                    here = slice((2 * chan + part) * frames, (2 * chan + part + 1) * frames)
                    rows.append(own[group, here, :])
                    for quarter in range(1, QUART):
                        total = own[quarter * groups + group, here, :].astype(jnp.float32)
                        before = late[(quarter - 1) * groups + group, here, :]
                        rows.append((total + before.astype(jnp.float32)).astype(jnp.bfloat16))
            pieces.append(jnp.concatenate(rows, axis=0))
    stacked = jnp.concatenate(pieces, axis=1)
    depth = stacked.shape[0] // pair
    contract = (((1,), (1,)), ((), ()))
    lane = lax.broadcasted_iota(jnp.int32, (tile, depth), 1)
    sign = jnp.where(lane < depth // 2, 1.0, -1.0)
    for first in range(0, inputs, tile):
        part = pl.ds(first, tile)
        result = lax.dot_general(
            pick[part, :], stacked, contract, preferred_element_type=jnp.float32
        )
        ordered[part, :] = result.astype(jnp.bfloat16)
        for chan in range(pair):
            lanes = slice(chan * depth, (chan + 1) * depth)
            swapped = pltpu.roll(result[:, lanes], depth // 2, 1) * sign
            turned[part, lanes] = swapped.astype(jnp.bfloat16)
    for chan in range(pair):
        lanes = slice(chan * depth, (chan + 1) * depth)
        for first in range(0, inputs, tile):
            left = ordered[first : first + tile, lanes]
            for other in range(0, inputs, tile):
                place = pl.ds(other, tile)
                if other >= first:
                    upper = lax.dot_general(
                        left, ordered[place, lanes], contract, preferred_element_type=jnp.float32
                    )
                if other <= first:
                    lower = lax.dot_general(
                        left, turned[place, lanes], contract, preferred_element_type=jnp.float32
                    )
                if other > first:
                    result = upper
                elif other < first:
                    result = lower
                else:
                    row = lax.broadcasted_iota(jnp.int32, (tile, tile), 0)
                    column = lax.broadcasted_iota(jnp.int32, (tile, tile), 1)
                    result = jnp.where(row <= column, upper, lower)
                out_ref[chan, first : first + tile, place] = (result * scale).astype(jnp.bfloat16)


def back(order, datas, each, sets, chan_dev, earlier):
    sources, both_rows, slots = datas[0].shape
    inputs = order.shape[1]
    groups = sources // QUART
    held = chan_dev // sets
    pair = 2 if held % 2 == 0 else 1
    steps = held // pair
    block_rows = both_rows // 2 // steps
    depth = QUART * block_rows // pair
    block_shape = (sources, block_rows, slots)
    operands = [order] + list(datas) + list(datas)
    in_specs = [pl.BlockSpec((1, inputs), lambda k: (0, 0))]
    in_specs += [pl.BlockSpec(block_shape, lambda k: (0, k, 0))] * len(datas)
    in_specs += [pl.BlockSpec(block_shape, lambda k: (0, steps + k, 0))] * len(datas)
    aliases = {}
    scale = 1.0 / (QUART * block_rows // (2 * pair))
    if earlier is not None:
        aliases = {len(operands): 0}
        operands.append(earlier)
        in_specs.append(pl.BlockSpec(memory_space=pl.ANY))
    return pl.pallas_call(
        functools.partial(back_kernel, len(datas), groups, pair, scale),
        grid=(steps,),
        in_specs=in_specs,
        out_specs=pl.BlockSpec((pair, inputs, inputs), lambda k: (k + each * steps, 0, 0)),
        out_shape=jax.ShapeDtypeStruct((chan_dev, inputs, inputs), jnp.bfloat16),
        scratch_shapes=[
            pltpu.VMEM((inputs, inputs), jnp.bfloat16),
            pltpu.VMEM((inputs, pair * depth), jnp.bfloat16),
            pltpu.VMEM((inputs, pair * depth), jnp.bfloat16),
        ],
        input_output_aliases=aliases,
        cost_estimate=pl.CostEstimate(
            flops=held * inputs * inputs * 1024,
            bytes_accessed=2 * held * inputs * inputs,
            transcendentals=0,
        ),
        name="back",
    )(*operands)


def on_device(samples, fir, chan_assign, input_order):
    own_frames = samples[0]
    frames, slots_dev, frame_len = own_frames.shape
    chan_count = lax.axis_size("chan")
    chan_dev = chan_assign.shape[0] // chan_count
    sets = 2 if chan_dev % 2 == 0 else 1
    held = chan_dev // sets
    blocks = 2 if slots_dev % (2 * LANES) == 0 else 1
    chans = chan_assign.reshape(chan_count, sets, held).transpose(1, 0, 2).reshape(-1)
    fine, coarse = split_table(chans, frame_len)
    order = input_order[None, :]

    ready = [[None] * blocks for _ in range(sets)]
    for block in range(blocks):
        parts = front(own_frames, fir, fine, coarse, block, blocks, sets, chan_count)
        for each in range(sets):
            ready[each][block] = lax.all_to_all(
                parts[each], "chan", split_axis=0, concat_axis=0, tiled=True
            )
    vis = None
    for each in range(sets):
        vis = back(order, ready[each], each, sets, chan_dev, vis)
    return vis


def solution(mesh):
    in_specs = (P(("grp", "chan"), None, None, None), P(), P(), P())
    out_specs = P(("grp", "chan"), None, None)
    return jax.shard_map(
        on_device, mesh=mesh, in_specs=in_specs, out_specs=out_specs, check_vma=False
    )
```

time: 267 us -> 255 us (0.955)
  blocking collectives: 0 us -> 106 us
  waiting for transfers between devices: 132 us -> 57.5 us
  other arithmetic: 25.2 us -> 1.49 us
  starting transfers between devices: 21 us -> 10 us
  Pallas kernels: 81.6 us -> 74.7 us
    all_to_all x0 -> x2, blocking collectives: none -> 106 us  [on_device(): lax.all_to_all(parts[each], 'chan', split_axis=0, concat_axis=0, tiled=True)]
    all_to_all x4 -> x2, waiting for transfers between devices: 132 us -> 57.5 us  [on_device(): lax.all_to_all(parts[each], 'chan', split_axis=0, concat_axis=0, tiled=True)]
    concatenate x4 -> x0, other arithmetic: 11.6 us -> none  [on_device(): jnp.concatenate([parts[part * sets + each].reshape(chan_count, per_dest,...]
    all_to_all x4 -> x2, starting transfers between devices: 21 us -> 10 us  [on_device(): lax.all_to_all(parts[each], 'chan', split_axis=0, concat_axis=0, tiled=True)]
    convert_element_type x4 -> x0, other arithmetic: 8.62 us -> none  [on_device(): ready[each][block] = (own + late).astype(jnp.bfloat16)]
    pallas_call x2, Pallas kernels: 29.9 us -> 25.1 us  [back(): pl.pallas_call(functools.partial(back_kernel, len(datas), groups, pair, s...]
    another operation x2, other arithmetic: 4.99 us -> 0.76 us  [the longest x1 0.75 us: split_table(): fine = jnp.stack([jnp.cos(fine) * norm_scale, jnp.sin(fine) * norm_scale])]
    slice x4 -> x0, local copies, waits for them, and re-layouts: 3.62 us -> none  [on_device(): late = got[:chan_count - group_count, per_dest:].astype(jnp.float32)]
  transfers between devices with their start and end apart: 4 -> 2, of which waited for: 4 -> 2; matrix products, arithmetic and copies ran while one was open for 6% -> 0% of each run, Pallas kernels for 15% -> 15%
where the time goes in v2:
time: 255 us; the launch traced here: 254 us
  blocking collectives  106 us (42%)
  Pallas kernels  74.7 us (29%)
  waiting for transfers between devices  57.5 us (23%)
  starting transfers between devices  10 us (4%)
  local copies, waits for them, and re-layouts  4.15 us (2%)
    all_to_all x2, blocking collectives, on_device(): lax.all_to_all(parts[each], 'chan', split_axis=0, concat_axis=0, tiled=True)  106 us
    all_to_all x2, waiting for transfers between devices, on_device(): lax.all_to_all(parts[each], 'chan', split_axis=0, concat_axis=0, tiled=True)  57.5 us
    pallas_call x2, Pallas kernels, front(): pl.pallas_call(functools.partial(front_kernel, sets), grid=(frame_len //...  49.6 us
    pallas_call x2, Pallas kernels, back(): pl.pallas_call(functools.partial(back_kernel, len(datas), groups, pair, s...  25.1 us
    all_to_all x2, starting transfers between devices, on_device(): lax.all_to_all(parts[each], 'chan', split_axis=0, concat_axis=0, tiled=True)  10 us
  transfers between devices with their start and end apart: 2, of which 2 were waited for; matrix products, arithmetic and copies ran while one was open for 0% of the time, Pallas kernels for 15%

profile of v2, /device:TPU:13, one launch (start us, length us, event | category | flops | bytes accessed | tf_op | source)
XLA Modules:
  0.0 253.9 jit_solution(10593021993803735722)
XLA Ops:
  0.0 0.8 reshape.285
  0.8 0.1 mul.117
  0.9 0.6 cosine_multiply_fusion
  1.5 0.1 fusion.10
  1.6 2.0 copy.8.coarse_ref
  3.6 0.8 pad_maximum_fusion.fine_ref
  4.4 24.8 %front.3 = (bf16[16,512,128]{2,1,0:T(8,128)(2,1)}, bf16[16,512,128]{2,1,0:T(8,128)(2,1)}) custom-call(bf16[16,256,1024]{2,1,0:T(8,128)(2,1)} %bitcast.6, f32[16,1024]{1,0:T(8,128)} %fir_ref.3, f32[2,256,128]{2,1,0:T(8,128)} %pad_maximum_fusion.fine_ref, f32[8,2,256,1]{3,2,1,0:T(8,128)} %copy.8.coarse_ref), custom_call_target="tpu_custom_call" | custom-call | flops 4294967296 | bytes 8388608 | tf_op jit(solution)/shard_map/front/pallas_call | solution.py:150
  29.1 53.9 %all_to_all.20.refs_2_.refs_4_ = bf16[16,512,128]{2,1,0:T(8,128)(2,1)} all-to-all(bf16[16,512,128]{2,1,0:T(8,128)(2,1)} %get-tuple-element.10), channel_id=1, replica_groups=mesh['grp'=2,'chan'=16] {'chan'}, dimensions={0} | all-to-all | bytes 4194304 | tf_op jit(solution)/shard_map/all_to_all | solution.py:302
  83.0 5.0 %all-to-all-start.3 = ((bf16[16,512,128]{2,1,0:T(8,128)(2,1)}), bf16[16,512,128]{2,1,0:T(8,128)(2,1)S(1)}, u32[]{:S(2)}, u32[]{:S(2)}) async-start(bf16[16,512,128]{2,1,0:T(8,128)(2,1)} %get-tuple-element.12), calls=%async_computation.3 | async-start | bytes 4194304 | tf_op jit(solution)/shard_map/all_to_all | solution.py:302
  88.0 24.8 %front.2 = (bf16[16,512,128]{2,1,0:T(8,128)(2,1)}, bf16[16,512,128]{2,1,0:T(8,128)(2,1)}) custom-call(bf16[16,256,1024]{2,1,0:T(8,128)(2,1)} %bitcast.7, f32[16,1024]{1,0:T(8,128)} %fir_ref.3, f32[2,256,128]{2,1,0:T(8,128)} %pad_maximum_fusion.fine_ref, f32[8,2,256,1]{3,2,1,0:T(8,128)} %copy.8.coarse_ref), custom_call_target="tpu_custom_call" | custom-call | flops 4294967296 | bytes 8388608 | tf_op jit(solution)/shard_map/front/pallas_call | solution.py:150
  112.8 22.6 %all-to-all-done.3.refs_2_.refs_4_ = bf16[16,512,128]{2,1,0:T(8,128)(2,1)S(1)} async-done(((bf16[16,512,128]{2,1,0:T(8,128)(2,1)}), bf16[16,512,128]{2,1,0:T(8,128)(2,1)S(1)}, u32[]{:S(2)}, u32[]{:S(2)}) %all-to-all-start.3) | async-done | bytes 2097184 | tf_op jit(solution)/shard_map/all_to_all | solution.py:302
  135.4 0.0 copy-start.1
  135.5 52.2 %all_to_all.21.refs_1_.refs_3_ = bf16[16,512,128]{2,1,0:T(8,128)(2,1)} all-to-all(bf16[16,512,128]{2,1,0:T(8,128)(2,1)} %get-tuple-element.11), channel_id=1, replica_groups=mesh['grp'=2,'chan'=16] {'chan'}, dimensions={0} | all-to-all | bytes 4194304 | tf_op jit(solution)/shard_map/all_to_all | solution.py:302
  187.6 0.0 copy-done.1
  187.6 5.0 %all-to-all-start = ((bf16[16,512,128]{2,1,0:T(8,128)(2,1)}), bf16[16,512,128]{2,1,0:T(8,128)(2,1)S(1)}, u32[]{:S(2)}, u32[]{:S(2)}) async-start(bf16[16,512,128]{2,1,0:T(8,128)(2,1)} %get-tuple-element.9), calls=%async_computation | async-start | bytes 4194304 | tf_op jit(solution)/shard_map/all_to_all | solution.py:302
  192.6 12.6 %back.2.refs_5_ = bf16[16,1024,1024]{2,1,0:T(8,128)(2,1)} custom-call(s32[1,1024]{1,0:T(1,128)} %bitcast.4, bf16[16,512,128]{2,1,0:T(8,128)(2,1)} %all_to_all.21.refs_1_.refs_3_, bf16[16,512,128]{2,1,0:T(8,128)(2,1)} %copy-done.1, bf16[16,512,128]{2,1,0:T(8,128)(2,1)} %all_to_all.21.refs_1_.refs_3_, bf16[16,512,128]{2,1,0:T(8,128)(2,1)} %copy-done.1), custom_call_target="tpu_custom_call" | custom-call | flops 8589934592 | bytes 16777216 | tf_op jit(solution)/shard_map/back/pallas_call | solution.py:265
  205.2 34.9 %all-to-all-done.refs_1_.refs_3_ = bf16[16,512,128]{2,1,0:T(8,128)(2,1)S(1)} async-done(((bf16[16,512,128]{2,1,0:T(8,128)(2,1)}), bf16[16,512,128]{2,1,0:T(8,128)(2,1)S(1)}, u32[]{:S(2)}, u32[]{:S(2)}) %all-to-all-start) | async-done | bytes 2097184 | tf_op jit(solution)/shard_map/all_to_all | solution.py:302
  240.1 0.0 copy-start
  240.1 1.3 copy-done
  241.4 12.5 %back.3 = bf16[16,1024,1024]{2,1,0:T(8,128)(2,1)} custom-call(s32[1,1024]{1,0:T(1,128)} %bitcast.5, bf16[16,512,128]{2,1,0:T(8,128)(2,1)} %copy-done, bf16[16,512,128]{2,1,0:T(8,128)(2,1)} %all_to_all.20.refs_2_.refs_4_, bf16[16,512,128]{2,1,0:T(8,128)(2,1)} %copy-done, ...), custom_call_target="tpu_custom_call", output_to_operand_aliasing={{}: (5, {})} | custom-call | flops 8589934592 | bytes 16777216 | tf_op jit(solution)/shard_map/back/pallas_call | solution.py:265
  (3 shorter events, 0.0 us)
Async XLA Ops:
  83.0 52.4 %all-to-all-start.3 = ((bf16[16,512,128]{2,1,0:T(8,128)(2,1)}), bf16[16,512,128]{2,1,0:T(8,128)(2,1)S(1)}, u32[]{:S(2)}, u32[]{:S(2)}) async-start(bf16[16,512,128]{2,1,0:T(8,128)(2,1)} %get-tuple-element.12), calls=%async_computation.3 | async-start | bytes 4194304 | tf_op jit(solution)/shard_map/all_to_all | solution.py:302
  135.4 52.2 %copy-start.1 = (bf16[16,512,128]{2,1,0:T(8,128)(2,1)}, bf16[16,512,128]{2,1,0:T(8,128)(2,1)S(1)}, u32[]{:S(2)}) copy-start(bf16[16,512,128]{2,1,0:T(8,128)(2,1)S(1)} %all-to-all-done.3.refs_2_.refs_4_) | copy-start | bytes 6291460
  187.6 52.4 %all-to-all-start = ((bf16[16,512,128]{2,1,0:T(8,128)(2,1)}), bf16[16,512,128]{2,1,0:T(8,128)(2,1)S(1)}, u32[]{:S(2)}, u32[]{:S(2)}) async-start(bf16[16,512,128]{2,1,0:T(8,128)(2,1)} %get-tuple-element.9), calls=%async_computation | async-start | bytes 4194304 | tf_op jit(solution)/shard_map/all_to_all | solution.py:302
  240.1 1.3 copy-start

commit v3 on v2

--- a/solution.py
+++ b/solution.py
@@ -7,6 +7,7 @@
 from jax.experimental import pallas as pl
 from jax.experimental.pallas import tpu as pltpu
 from jax.sharding import PartitionSpec as P
+
 
 QUART = 4
 LANES = 128
@@ -60,8 +61,9 @@
     return outs + high[half - 1 :]
 
 
-def front_kernel(sets, x_ref, fir_ref, fine_ref, coarse_ref, *rest):
-    outs, (filt, spread, table, coeffs) = rest[:sets], rest[sets:]
+def front_kernel(groups, x_ref, fir_ref, fine_ref, coarse_ref, *rest):
+    outs, (filt, table, coeffs, spread) = rest[:-4], rest[-4:]
+    sets = sum(len(members) for members, _ in groups)
     frames, slots, lanes = x_ref.shape
     taps = fir_ref.shape[0]
     step = pl.program_id(0)
@@ -108,47 +110,73 @@
 
     lax.fori_loop(0, slots // 16, filter_rows, 0)
 
+    def deliver(part, each, which, values):
+        first = 0
+        for members, whole in groups:
+            refs = outs[first : first + (1 if whole else 2 * QUART)]
+            first += len(refs)
+            if each not in members:
+                continue
+            if whole:
+                dests, _, per_dest = refs[0].shape[:3]
+                refs[0][:, part, :, which] = values.reshape(dests, per_dest, frames, slots)
+            else:
+                _, plane, per_dest = refs[0].shape[:3]
+                values = values.reshape(QUART, plane, per_dest, frames, slots)
+                for target in range(QUART):
+                    out = refs[part * QUART + target]
+                    out[members.index(each), :, :, which] = values[target]
+
     @pl.when(step == pl.num_programs(0) - 1)
     def _():
-        pair = 2 if slots % LANES == 0 else 1
+        contract = (((1,), (1,)), ((), ()))
         for part in range(2):
-
-            def transform(index, carry):
-                frame = index * pair
-                block = filt[pl.ds(part * frames + frame, pair)]
+            if slots % LANES == 0:
                 result = lax.dot_general(
                     table[...],
-                    block.reshape(pair * slots, -1),
-                    (((1,), (1,)), ((), ())),
+                    filt[part * frames : (part + 1) * frames].reshape(frames * slots, -1),
+                    contract,
                     preferred_element_type=jnp.float32,
                 )
-                for one in range(pair):
-                    for piece in range(2 * sets):
-                        each, which = divmod(piece, 2)
-                        start = each * held * 2 * frames + which * frames
-                        spread[pl.ds(start + frame + one, held, stride=2 * frames), :] = result[
-                            piece * held : (piece + 1) * held, one * slots : (one + 1) * slots
-                        ]
-                return carry
-
-            lax.fori_loop(0, frames // pair, transform, 0)
-            for each in range(sets):
-                dests, both_rows, _ = outs[each].shape
-                per_dest = both_rows // 2
-                block = spread[each * dests * per_dest : (each + 1) * dests * per_dest, :]
-                outs[each][:, part * per_dest : (part + 1) * per_dest, :] = block.reshape(
-                    dests, per_dest, slots
-                ).astype(jnp.bfloat16)
-
-
-def front(x, fir, fine, coarse, block, blocks, sets, dests):
+                result = result.reshape(-1, frames, slots)
+                for piece in range(2 * sets):
+                    values = result[piece * held : (piece + 1) * held].astype(jnp.bfloat16)
+                    deliver(part, piece // 2, piece % 2, values)
+            else:
+
+                def transform(frame, carry):
+                    result = lax.dot_general(
+                        table[...],
+                        filt[part * frames + frame],
+                        contract,
+                        preferred_element_type=jnp.float32,
+                    )
+                    spread[pl.ds(frame, 2 * chans, stride=frames), :] = result
+                    return carry
+
+                lax.fori_loop(0, frames, transform, 0)
+                for piece in range(2 * sets):
+                    values = spread[piece * held * frames : (piece + 1) * held * frames, :]
+                    values = values.astype(jnp.bfloat16).reshape(held, frames, slots)
+                    deliver(part, piece // 2, piece % 2, values)
+
+
+def front(x, fir, fine, coarse, block, blocks, groups, dests):
     frames, slots_dev, frame_len = x.shape
     slots = slots_dev // blocks
     taps = fir.shape[0]
     chans = fine.shape[1]
-    out_shape = (dests, chans // sets // dests * 4 * frames, slots)
+    sets = sum(len(members) for members, _ in groups)
+    tail = (chans // sets // dests, 2, frames, slots)
+    shapes = []
+    for members, whole in groups:
+        if whole:
+            shapes += [(dests, 2, tail[0], *tail[1:])]
+        else:
+            shapes += [(len(members), dests // QUART, *tail)] * (2 * QUART)
+    spread = (8, LANES) if slots % LANES == 0 else (2 * chans * frames, slots)
     return pl.pallas_call(
-        functools.partial(front_kernel, sets),
+        functools.partial(front_kernel, groups),
         grid=(frame_len // LANES,),
         in_specs=[
             pl.BlockSpec((frames, slots, LANES), lambda j: (0, block, j)),
@@ -156,14 +184,16 @@
             pl.BlockSpec(fine.shape, lambda j: (0, 0, 0), pipeline_mode=pl.Buffered(1)),
             pl.BlockSpec((1, 2, chans, 1), lambda j: (j, 0, 0, 0)),
         ],
-        out_specs=[pl.BlockSpec(out_shape, lambda j: (0, 0, 0), pipeline_mode=pl.Buffered(1))]
-        * sets,
-        out_shape=[jax.ShapeDtypeStruct(out_shape, jnp.bfloat16)] * sets,
+        out_specs=[
+            pl.BlockSpec(shape, lambda j: (0, 0, 0, 0, 0, 0), pipeline_mode=pl.Buffered(1))
+            for shape in shapes
+        ],
+        out_shape=[jax.ShapeDtypeStruct(shape, jnp.bfloat16) for shape in shapes],
         scratch_shapes=[
             pltpu.VMEM((2 * frames, slots, frame_len), jnp.bfloat16),
-            pltpu.VMEM((2 * chans * frames, slots), jnp.float32),
             pltpu.VMEM((2 * chans, frame_len), jnp.bfloat16),
             pltpu.VMEM((4 * taps, LANES), jnp.float32),
+            pltpu.VMEM(spread, jnp.float32),
         ],
         cost_estimate=pl.CostEstimate(
             flops=8 * frames * slots * frame_len * chans,
@@ -174,11 +204,70 @@
     )(x, fir, fine, coarse)
 
 
-def back_kernel(blocks, groups, pair, scale, *refs):
-    order_ref, owns, lates = refs[0], refs[1 : 1 + blocks], refs[1 + blocks : 1 + 2 * blocks]
+def meet_kernel(sets, where_ref, *refs):
+    owns, lates = refs[:QUART], refs[QUART : 2 * QUART]
+    risen, fallen = refs[2 * QUART : 3 * QUART - 1], refs[3 * QUART - 1 : 4 * QUART - 2]
+    outs, side = refs[4 * QUART - 2 : -1], refs[-1]
+    here = where_ref[0]
+
+    def add(one, other):
+        return (one.astype(jnp.float32) + other.astype(jnp.float32)).astype(jnp.bfloat16)
+
+    for target in range(QUART):
+
+        @pl.when(here <= target)
+        def _():
+            for each in range(sets):
+                own = owns[target][each, 0]
+                outs[each][target, 0] = add(own, risen[target - 1][each, 0]) if target else own
+
+        if target == QUART - 1:
+            continue
+
+        @pl.when(here > target)
+        def _():
+            for each in range(sets):
+                outs[each][target, 0] = add(fallen[target][each, 0], lates[target][each, 0])
+
+        @pl.when(here == target)
+        def _():
+            for each in range(sets):
+                side[0, each] = add(fallen[target][each, 0], lates[target][each, 0])
+
+    @pl.when(here == QUART - 1)
+    def _():
+        side[...] = jnp.zeros_like(side)
+
+
+def meet(quarter, owns, lates, risen, fallen):
+    sets, plane, *tail = owns[0].shape
+    block = pl.BlockSpec((sets, 1, *tail), lambda g, _: (0, g, 0, 0, 0, 0))
+    out = pl.BlockSpec((QUART, 1, *tail), lambda g, _: (0, g, 0, 0, 0, 0))
+    side = pl.BlockSpec((1, sets, *tail), lambda g, _: (g, 0, 0, 0, 0, 0))
+    shapes = [(QUART, plane, *tail)] * sets + [(plane, sets, *tail)]
+    operands = [*owns, *lates, *risen, *fallen]
+    return pl.pallas_call(
+        functools.partial(meet_kernel, sets),
+        grid_spec=pltpu.PrefetchScalarGridSpec(
+            num_scalar_prefetch=1,
+            grid=(plane,),
+            in_specs=[block] * len(operands),
+            out_specs=[out] * sets + [side],
+        ),
+        out_shape=[jax.ShapeDtypeStruct(shape, jnp.bfloat16) for shape in shapes],
+        cost_estimate=pl.CostEstimate(
+            flops=sets * owns[0].size * 5, bytes_accessed=owns[0].size * 40, transcendentals=0
+        ),
+        name="meet",
+    )(quarter, *operands)
+
+
+def back_kernel(kinds, groups, pair, scale, where_ref, order_ref, *refs):
+    firsts, seconds = refs[: len(kinds)], refs[len(kinds) : 2 * len(kinds)]
     out_ref, pick, ordered, turned = refs[-4:]
     inputs = out_ref.shape[-1]
     tile = min(256, inputs)
+    here = where_ref[0]
 
     @pl.when(pl.program_id(0) == 0)
     def _():
@@ -187,20 +276,29 @@
             hit = jnp.where(order_ref[...] == wanted, 1.0, 0.0)
             pick[first : first + tile, :] = hit.astype(jnp.bfloat16)
 
-    per_chan = owns[0].shape[1] // pair
-    frames = per_chan // 2
+    def rows_of(kind, first, second, group, place, chan, part):
+        if kind == "whole":
+            if place == 0:
+                return first[group, 0, chan, part]
+            quarter = jnp.where(place <= here, place, place + 1)
+            if place == QUART - 1:
+                quarter = jnp.minimum(here + 1, QUART - 1)
+            own = first[quarter * groups + group, 0, chan, part].astype(jnp.float32)
+            before = second[(quarter - 1) * groups + group, 0, chan, part].astype(jnp.float32)
+            return (own + before).astype(jnp.bfloat16)
+        value = first[place * groups + group, chan, part]
+        if place == QUART - 1:
+            value = jnp.where(here < QUART - 1, second[group, 0, chan, part], value)
+        return value
+
     pieces = []
     for group in range(groups):
-        for own, late in zip(owns, lates):
+        for kind, first, second in zip(kinds, firsts, seconds):
             rows = []
             for chan in range(pair):
                 for part in range(2):
-                    here = slice((2 * chan + part) * frames, (2 * chan + part + 1) * frames)
-                    rows.append(own[group, here, :])
-                    for quarter in range(1, QUART):
-                        total = own[quarter * groups + group, here, :].astype(jnp.float32)
-                        before = late[(quarter - 1) * groups + group, here, :]
-                        rows.append((total + before.astype(jnp.float32)).astype(jnp.bfloat16))
+                    for place in range(QUART):
+                        rows.append(rows_of(kind, first, second, group, place, chan, part))
             pieces.append(jnp.concatenate(rows, axis=0))
     stacked = jnp.concatenate(pieces, axis=1)
     depth = stacked.shape[0] // pair
@@ -242,37 +340,56 @@
                 out_ref[chan, first : first + tile, place] = (result * scale).astype(jnp.bfloat16)
 
 
-def back(order, datas, each, sets, chan_dev, earlier):
-    sources, both_rows, slots = datas[0].shape
+def back(quarter, order, datas, each, sets, chan_dev, earlier):
     inputs = order.shape[1]
-    groups = sources // QUART
     held = chan_dev // sets
     pair = 2 if held % 2 == 0 else 1
     steps = held // pair
-    block_rows = both_rows // 2 // steps
-    depth = QUART * block_rows // pair
-    block_shape = (sources, block_rows, slots)
-    operands = [order] + list(datas) + list(datas)
-    in_specs = [pl.BlockSpec((1, inputs), lambda k: (0, 0))]
-    in_specs += [pl.BlockSpec(block_shape, lambda k: (0, k, 0))] * len(datas)
-    in_specs += [pl.BlockSpec(block_shape, lambda k: (0, steps + k, 0))] * len(datas)
+    sources, (frames, slots) = datas[0][1].shape[0], datas[0][1].shape[-2:]
+    groups = sources // QUART
+    tail = (pair, 2, frames, slots)
+    depth = QUART * 2 * frames
+    firsts, seconds, first_specs, second_specs = [], [], [], []
+    for kind, *arrays in datas:
+        firsts.append(arrays[0])
+        if kind == "whole":
+            seconds.append(arrays[0])
+            for part, specs in ((0, first_specs), (1, second_specs)):
+                specs.append(
+                    pl.BlockSpec((sources, 1, *tail), lambda k, _, part=part: (0, part, k, 0, 0, 0))
+                )
+        else:
+            seconds.append(arrays[1])
+            member = arrays[2]
+            first_specs.append(pl.BlockSpec((sources, *tail), lambda k, _: (0, k, 0, 0, 0)))
+            second_specs.append(
+                pl.BlockSpec(
+                    (groups, 1, *tail), lambda k, _, member=member: (0, member, k, 0, 0, 0)
+                )
+            )
+    operands = [quarter, order, *firsts, *seconds]
+    in_specs = [pl.BlockSpec((1, inputs), lambda k, _: (0, 0)), *first_specs, *second_specs]
     aliases = {}
-    scale = 1.0 / (QUART * block_rows // (2 * pair))
+    scale = 1.0 / (QUART * frames)
     if earlier is not None:
         aliases = {len(operands): 0}
         operands.append(earlier)
         in_specs.append(pl.BlockSpec(memory_space=pl.ANY))
+    kinds = tuple(data[0] for data in datas)
     return pl.pallas_call(
-        functools.partial(back_kernel, len(datas), groups, pair, scale),
-        grid=(steps,),
-        in_specs=in_specs,
-        out_specs=pl.BlockSpec((pair, inputs, inputs), lambda k: (k + each * steps, 0, 0)),
+        functools.partial(back_kernel, kinds, groups, pair, scale),
+        grid_spec=pltpu.PrefetchScalarGridSpec(
+            num_scalar_prefetch=1,
+            grid=(steps,),
+            in_specs=in_specs,
+            out_specs=pl.BlockSpec((pair, inputs, inputs), lambda k, _: (k + each * steps, 0, 0)),
+            scratch_shapes=[
+                pltpu.VMEM((inputs, inputs), jnp.bfloat16),
+                pltpu.VMEM((inputs, pair * depth), jnp.bfloat16),
+                pltpu.VMEM((inputs, pair * depth), jnp.bfloat16),
+            ],
+        ),
         out_shape=jax.ShapeDtypeStruct((chan_dev, inputs, inputs), jnp.bfloat16),
-        scratch_shapes=[
-            pltpu.VMEM((inputs, inputs), jnp.bfloat16),
-            pltpu.VMEM((inputs, pair * depth), jnp.bfloat16),
-            pltpu.VMEM((inputs, pair * depth), jnp.bfloat16),
-        ],
         input_output_aliases=aliases,
         cost_estimate=pl.CostEstimate(
             flops=held * inputs * inputs * 1024,
@@ -283,10 +400,31 @@
     )(*operands)
 
 
+def hops(values, plane, upward):
+    moved = []
+    for target, value in values:
+        if upward:
+            senders, step = range(target), plane
+        else:
+            senders, step = range(target + 1, QUART), -plane
+        places = [quarter * plane + i for quarter in senders for i in range(plane)]
+        moved.append(lax.ppermute(value, "chan", [(place, place + step) for place in places]))
+    return moved
+
+
+def after(value, earlier):
+    return lax.optimization_barrier((value, earlier))[0]
+
+
+def exchange(value):
+    return lax.all_to_all(value, "chan", split_axis=0, concat_axis=0, tiled=True)
+
+
 def on_device(samples, fir, chan_assign, input_order):
     own_frames = samples[0]
-    frames, slots_dev, frame_len = own_frames.shape
+    _, slots_dev, frame_len = own_frames.shape
     chan_count = lax.axis_size("chan")
+    plane = chan_count // QUART
     chan_dev = chan_assign.shape[0] // chan_count
     sets = 2 if chan_dev % 2 == 0 else 1
     held = chan_dev // sets
@@ -294,23 +432,59 @@
     chans = chan_assign.reshape(chan_count, sets, held).transpose(1, 0, 2).reshape(-1)
     fine, coarse = split_table(chans, frame_len)
     order = input_order[None, :]
+    quarter = (lax.axis_index("chan") // plane).astype(jnp.int32)[None]
+    planes = [[q * plane + i for i in range(plane)] for q in range(QUART)]
 
     ready = [[None] * blocks for _ in range(sets)]
+    source, token, pending = own_frames, None, []
     for block in range(blocks):
-        parts = front(own_frames, fir, fine, coarse, block, blocks, sets, chan_count)
-        for each in range(sets):
-            ready[each][block] = lax.all_to_all(
-                parts[each], "chan", split_axis=0, concat_axis=0, tiled=True
-            )
+        if block == 0:
+            groups = [((0,), True)] + [((each,), False) for each in range(1, sets)]
+        else:
+            groups = [(tuple(range(sets)), False)]
+        parts = front(source, fir, fine, coarse, block, blocks, groups, chan_count)
+        source = after(own_frames, parts[0])
+        for members, whole in groups:
+            if whole:
+                token = exchange(parts[0])
+                ready[members[0]][block] = ("whole", token)
+                parts = parts[1:]
+                continue
+            owns, lates, parts = parts[:QUART], parts[QUART : 2 * QUART], parts[2 * QUART :]
+            risen = hops(list(enumerate(lates))[1:], plane, True)
+            fallen = hops(list(enumerate(owns))[:-1], plane, False)
+            pending.append((block, members, owns, lates, risen, fallen))
+    for block, members, owns, lates, risen, fallen in pending:
+        *met, side = meet(quarter, [after(owns[0], token), *owns[1:]], lates, risen, fallen)
+        swapped = []
+        for index in range(len(members)):
+            block_met = met[index].reshape(chan_count, *met[index].shape[2:])
+            if index:
+                block_met = after(block_met, side)
+            token = exchange(block_met)
+            swapped.append(token)
+            if index == 0:
+                side = lax.all_to_all(
+                    after(side, token),
+                    "chan",
+                    split_axis=0,
+                    concat_axis=0,
+                    axis_index_groups=planes,
+                    tiled=True,
+                )
+        for index, each in enumerate(members):
+            ready[each][block] = ("met", swapped[index], side, index)
     vis = None
     for each in range(sets):
-        vis = back(order, ready[each], each, sets, chan_dev, vis)
+        vis = back(quarter, order, ready[each], each, sets, chan_dev, vis)
     return vis
 
 
 def solution(mesh):
     in_specs = (P(("grp", "chan"), None, None, None), P(), P(), P())
     out_specs = P(("grp", "chan"), None, None)
+
+
     return jax.shard_map(
         on_device, mesh=mesh, in_specs=in_specs, out_specs=out_specs, check_vma=False
     )

time: 255 us -> 262 us (1.027)
  blocking collectives: 106 us -> 30.3 us
  waiting for transfers between devices: 57.5 us -> 104 us
  starting transfers between devices: 10 us -> 50.1 us
  Pallas kernels: 74.7 us -> 70.5 us
    ppermute x0 -> x12, waiting for transfers between devices: none -> 80 us  [hops(): lax.ppermute(value, 'chan', [(place, place + step) for place in places])]
    all_to_all x2 -> x1, blocking collectives: 106 us -> 30.3 us  [exchange(): lax.all_to_all(value, 'chan', split_axis=0, concat_axis=0, tiled=True)]
    all_to_all x2 -> x5, waiting for transfers between devices: 57.5 us -> 23.9 us  [the longest x3 12.4 us: exchange(): lax.all_to_all(value, 'chan', split_axis=0, concat_axis=0, tiled=True)]
    ppermute x0 -> x12, starting transfers between devices: none -> 22.7 us  [hops(): lax.ppermute(value, 'chan', [(place, place + step) for place in places])]
    all_to_all x2 -> x5, starting transfers between devices: 10 us -> 27.4 us  [the longest x3 18.6 us: exchange(): lax.all_to_all(value, 'chan', split_axis=0, concat_axis=0, tiled=True)]
    pallas_call x4 -> x6, Pallas kernels: 74.7 us -> 70.5 us  [the longest x2 36.4 us: front(): pl.pallas_call(functools.partial(front_kernel, groups), grid=(frame_len /...]
  transfers between devices with their start and end apart: 2 -> 17, of which waited for: 2 -> 10; matrix products, arithmetic and copies ran while one was open for 0% -> 0% of each run, Pallas kernels for 15% -> 12%
where the time goes in v3:
time: 262 us; the launch traced here: 260 us
  waiting for transfers between devices  104 us (40%)
  Pallas kernels  70.5 us (27%)
  starting transfers between devices  50.1 us (19%)
  blocking collectives  30.3 us (12%)
  local copies, waits for them, and re-layouts  3.87 us (1%)
    ppermute x12, waiting for transfers between devices, hops(): lax.ppermute(value, 'chan', [(place, place + step) for place in places])  80 us
    pallas_call x2, Pallas kernels, front(): pl.pallas_call(functools.partial(front_kernel, groups), grid=(frame_len /...  36.4 us
    all_to_all x1, blocking collectives, exchange(): lax.all_to_all(value, 'chan', split_axis=0, concat_axis=0, tiled=True)  30.3 us
    pallas_call x2, Pallas kernels, back(): pl.pallas_call(functools.partial(back_kernel, kinds, groups, pair, scale)...  24.7 us
    ppermute x12, starting transfers between devices, hops(): lax.ppermute(value, 'chan', [(place, place + step) for place in places])  22.7 us
    all_to_all x3, starting transfers between devices, exchange(): lax.all_to_all(value, 'chan', split_axis=0, concat_axis=0, tiled=True)  18.6 us
    all_to_all x3, waiting for transfers between devices, exchange(): lax.all_to_all(value, 'chan', split_axis=0, concat_axis=0, tiled=True)  12.4 us
    all_to_all x2, waiting for transfers between devices, on_device(): lax.all_to_all(after(side, token), 'chan', split_axis=0, concat_axis=0, a...  11.5 us
  transfers between devices with their start and end apart: 17, of which 10 were waited for; matrix products, arithmetic and copies ran while one was open for 0% of the time, Pallas kernels for 12%

profile of v3, /device:TPU:13, one launch (start us, length us, event | category | flops | bytes accessed | tf_op | source)
XLA Modules:
  0.0 260.4 jit_solution(8591851754903844568)
XLA Ops:
  0.0 0.8 reshape.294
  0.8 0.1 mul.117
  0.9 0.6 cosine_multiply_fusion
  1.5 0.1 fusion.10
  1.6 2.0 copy.8.coarse_ref
  3.6 0.7 pad_maximum_fusion.fine_ref
  4.3 18.1 %front.2 = (bf16[16,2,8,2,16,128]{5,4,3,2,1,0:T(8,128)(2,1)}, bf16[1,4,8,2,16,128]{5,4,3,2,1,0:T(8,128)(2,1)}, bf16[1,4,8,2,16,128]{5,4,3,2,1,0:T(8,128)(2,1)}, ...) custom-call(bf16[16,256,1024]{2,1,0:T(8,128)(2,1)} %bitcast.13, ...), custom_call_target="tpu_custom_call" | custom-call | flops 4294967296 | bytes 8388608 | tf_op jit(solution)/shard_map/front/pallas_call | solution.py:178
  22.4 6.5 %all-to-all-start = ((bf16[16,2,8,2,16,128]{5,4,3,2,1,0:T(8,128)(2,1)}), bf16[16,2,8,2,16,128]{5,4,3,2,1,0:T(8,128)(2,1)S(1)}, u32[]{:S(2)}, u32[]{:S(2)}) async-start(bf16[16,2,8,2,16,128]{5,4,3,2,1,0:T(8,128)(2,1)} %get-tuple-element.34), calls=%async_computation | async-start | bytes 4194304 | tf_op jit(solution)/shard_map/all_to_all | solution.py:420
  29.0 2.2 collective-permute-start.3
  31.2 1.3 collective-permute-start.4
  32.5 0.7 collective-permute-start.5
  33.1 1.3 collective-permute-start
  34.4 4.0 %collective-permute-start.1 = (bf16[1,4,8,2,16,128]{5,4,3,2,1,0:T(8,128)(2,1)}, bf16[1,4,8,2,16,128]{5,4,3,2,1,0:T(8,128)(2,1)S(1)}, u32[]{:S(2)}, u32[]{:S(2)}) collective-permute-start(bf16[1,4,8,2,16,128]{5,4,3,2,1,0:T(8,128)(2,1)} %get-tuple-element.41.refs_6_), channel_id=1, source_target_pairs={{0,4},{1,5},{2,6},{3,7},{4,8},{5,9},{6,10},{7,11},{16,20},{17,21},... | collective-permute-start | bytes 786440 | tf_op jit(solution)/shard_map/ppermute | solution.py:411
  38.4 43.3 %collective-permute-done.3.refs_11_ = bf16[1,4,8,2,16,128]{5,4,3,2,1,0:T(8,128)(2,1)S(1)} collective-permute-done((bf16[1,4,8,2,16,128]{5,4,3,2,1,0:T(8,128)(2,1)}, bf16[1,4,8,2,16,128]{5,4,3,2,1,0:T(8,128)(2,1)S(1)}, u32[]{:S(2)}, u32[]{:S(2)}) %collective-permute-start.3) | collective-permute-done | bytes 262176 | tf_op jit(solution)/shard_map/ppermute | solution.py:411
  81.7 1.9 collective-permute-start.2
  83.7 0.0 all-to-all-done.refs_0_.refs_2_
  83.7 3.7 %collective-permute-done.4.refs_12_ = bf16[1,4,8,2,16,128]{5,4,3,2,1,0:T(8,128)(2,1)S(1)} collective-permute-done((bf16[1,4,8,2,16,128]{5,4,3,2,1,0:T(8,128)(2,1)}, bf16[1,4,8,2,16,128]{5,4,3,2,1,0:T(8,128)(2,1)S(1)}, u32[]{:S(2)}, u32[]{:S(2)}) %collective-permute-start.4) | collective-permute-done | bytes 262176 | tf_op jit(solution)/shard_map/ppermute | solution.py:411
  87.4 0.0 collective-permute-done.5.refs_13_
  87.4 0.0 collective-permute-done.refs_8_
  87.4 0.0 collective-permute-done.1.refs_9_
  87.4 2.9 %collective-permute-done.2.refs_10_ = bf16[1,4,8,2,16,128]{5,4,3,2,1,0:T(8,128)(2,1)} collective-permute-done((bf16[1,4,8,2,16,128]{5,4,3,2,1,0:T(8,128)(2,1)}, bf16[1,4,8,2,16,128]{5,4,3,2,1,0:T(8,128)(2,1)}, u32[]{:S(2)}, u32[]{:S(2)}) %collective-permute-start.2) | collective-permute-done | bytes 262176 | tf_op jit(solution)/shard_map/ppermute | solution.py:411
  90.3 4.1 %meet.2 = (bf16[4,4,8,2,16,128]{5,4,3,2,1,0:T(8,128)(2,1)}, bf16[4,1,8,2,16,128]{5,4,3,2,1,0:T(8,128)(2,1)}) custom-call(s32[1]{0:T(128)} %bitcast.where_ref, bf16[1,4,8,2,16,128]{5,4,3,2,1,0:T(8,128)(2,1)} %get-tuple-element.35.refs_0_, bf16[1,4,8,2,16,128]{5,4,3,2,1,0:T(8,128)(2,1)} %get-tuple-element.36.refs_1_, ...), custom_call_target="tpu_custom_call" | custom-call | flops 655360 | bytes 5242880 | tf_op jit(solution)/shard_map/meet/pallas_call | solution.py:249
  94.4 6.2 %all-to-all-start.1 = ((bf16[16,8,2,16,128]{4,3,2,1,0:T(8,128)(2,1)}), bf16[16,8,2,16,128]{4,3,2,1,0:T(8,128)(2,1)S(1)}, u32[]{:S(2)}, u32[]{:S(2)}) async-start(bf16[16,8,2,16,128]{4,3,2,1,0:T(8,128)(2,1)} %bitcast.7), calls=%async_computation.1 | async-start | bytes 2097152 | tf_op jit(solution)/shard_map/all_to_all | solution.py:420
  100.6 18.2 %front.3 = (bf16[2,4,8,2,16,128]{5,4,3,2,1,0:T(8,128)(2,1)}, bf16[2,4,8,2,16,128]{5,4,3,2,1,0:T(8,128)(2,1)}, bf16[2,4,8,2,16,128]{5,4,3,2,1,0:T(8,128)(2,1)}, b...) custom-call(bf16[16,256,1024]{2,1,0:T(8,128)(2,1)} %bitcast.14, ...), custom_call_target="tpu_custom_call" | custom-call | flops 4294967296 | bytes 8388608 | tf_op jit(solution)/shard_map/front/pallas_call | solution.py:178
  118.8 2.2 collective-permute-start.9
  121.0 1.3 collective-permute-start.10
  122.3 0.7 collective-permute-start.11
  123.0 1.3 collective-permute-start.6
  124.3 4.0 %collective-permute-start.7 = (bf16[2,4,8,2,16,128]{5,4,3,2,1,0:T(8,128)(2,1)}, bf16[2,4,8,2,16,128]{5,4,3,2,1,0:T(8,128)(2,1)}, u32[]{:S(2)}, u32[]{:S(2)}) collective-permute-start(bf16[2,4,8,2,16,128]{5,4,3,2,1,0:T(8,128)(2,1)} %get-tuple-element.52.refs_6_), channel_id=1, source_target_pairs={{0,4},{1,5},{2,6},{3,7},{4,8},{5,9},{6,10},{7,11},{16,20},{17,21},... | collective-permute-start | bytes 1572872 | tf_op jit(solution)/shard_map/ppermute | solution.py:411
  128.3 8.1 %collective-permute-done.9.refs_11_ = bf16[2,4,8,2,16,128]{5,4,3,2,1,0:T(8,128)(2,1)S(1)} collective-permute-done((bf16[2,4,8,2,16,128]{5,4,3,2,1,0:T(8,128)(2,1)}, bf16[2,4,8,2,16,128]{5,4,3,2,1,0:T(8,128)(2,1)S(1)}, u32[]{:S(2)}, u32[]{:S(2)}) %collective-permute-start.9) | collective-permute-done | bytes 524320 | tf_op jit(solution)/shard_map/ppermute | solution.py:411
  136.4 1.9 collective-permute-start.8
  138.3 0.0 all-to-all-done.1.refs_0_
  138.4 9.4 %collective-permute-done.10.refs_12_ = bf16[2,4,8,2,16,128]{5,4,3,2,1,0:T(8,128)(2,1)S(1)} collective-permute-done((bf16[2,4,8,2,16,128]{5,4,3,2,1,0:T(8,128)(2,1)}, bf16[2,4,8,2,16,128]{5,4,3,2,1,0:T(8,128)(2,1)S(1)}, u32[]{:S(2)}, u32[]{:S(2)}) %collective-permute-start.10) | collective-permute-done | bytes 524320 | tf_op jit(solution)/shard_map/ppermute | solution.py:411
  147.8 0.0 collective-permute-done.11.refs_13_
  147.8 0.0 collective-permute-done.6.refs_8_
  147.8 1.5 collective-permute-done.7.refs_9_
  149.3 11.2 %collective-permute-done.8.refs_10_ = bf16[2,4,8,2,16,128]{5,4,3,2,1,0:T(8,128)(2,1)} collective-permute-done((bf16[2,4,8,2,16,128]{5,4,3,2,1,0:T(8,128)(2,1)}, bf16[2,4,8,2,16,128]{5,4,3,2,1,0:T(8,128)(2,1)}, u32[]{:S(2)}, u32[]{:S(2)}) %collective-permute-start.8) | collective-permute-done | bytes 524320 | tf_op jit(solution)/shard_map/ppermute | solution.py:411
  160.5 5.3 %meet.3 = (bf16[4,4,8,2,16,128]{5,4,3,2,1,0:T(8,128)(2,1)}, bf16[4,4,8,2,16,128]{5,4,3,2,1,0:T(8,128)(2,1)}, bf16[4,2,8,2,16,128]{5,4,3,2,1,0:T(8,128)(2,1)}) custom-call(s32[1]{0:T(128)} %bitcast.where_ref, bf16[2,4,8,2,16,128]{5,4,3,2,1,0:T(8,128)(2,1)} %get-tuple-element.46.refs_0_, bf16[2,4,8,2,16,128]{5,4,3,2,1,0:T(8,128)(2,1)} %get-tuple-element.47.refs_1_, ...), custom_call_target="tpu_custom_call" | custom-call | flops 2621440 | bytes 10485760 | tf_op jit(solution)/shard_map/meet/pallas_call | solution.py:249
  165.9 30.3 %all_to_all.30.refs_1_ = bf16[16,8,2,16,128]{4,3,2,1,0:T(8,128)(2,1)} all-to-all(bf16[16,8,2,16,128]{4,3,2,1,0:T(8,128)(2,1)} %bitcast.9), channel_id=1, replica_groups=mesh['grp'=2,'chan'=16] {'chan'}, dimensions={0} | all-to-all | bytes 2097152 | tf_op jit(solution)/shard_map/all_to_all | solution.py:420
  196.2 3.9 %all-to-all-start.3 = ((bf16[4,2,8,2,16,128]{5,4,3,2,1,0:T(8,128)(2,1)}), bf16[4,2,8,2,16,128]{5,4,3,2,1,0:T(8,128)(2,1)S(1)}, u32[]{:S(2)}, u32[]{:S(2)}) async-start(bf16[4,2,8,2,16,128]{5,4,3,2,1,0:T(8,128)(2,1)} %get-tuple-element.57), calls=%async_computation.3 | async-start | bytes 1048576 | tf_op jit(solution)/shard_map/all_to_all | solution.py:467
  200.1 7.3 %all-to-all-done.3.refs_3_ = bf16[4,2,8,2,16,128]{5,4,3,2,1,0:T(8,128)(2,1)S(1)} async-done(((bf16[4,2,8,2,16,128]{5,4,3,2,1,0:T(8,128)(2,1)}), bf16[4,2,8,2,16,128]{5,4,3,2,1,0:T(8,128)(2,1)S(1)}, u32[]{:S(2)}, u32[]{:S(2)}) %all-to-all-start.3) | async-done | bytes 524320 | tf_op jit(solution)/shard_map/all_to_all | solution.py:467
  207.4 4.9 %all-to-all-start.5 = ((bf16[4,1,8,2,16,128]{5,4,3,2,1,0:T(8,128)(2,1)}), bf16[4,1,8,2,16,128]{5,4,3,2,1,0:T(8,128)(2,1)S(1)}, u32[]{:S(2)}, u32[]{:S(2)}) async-start(bf16[4,1,8,2,16,128]{5,4,3,2,1,0:T(8,128)(2,1)} %get-tuple-element.60), calls=%async_computation.5 | async-start | bytes 524288 | tf_op jit(solution)/shard_map/all_to_all | solution.py:467
  212.3 4.2 %all-to-all-done.5.refs_2_ = bf16[4,1,8,2,16,128]{5,4,3,2,1,0:T(8,128)(2,1)S(1)} async-done(((bf16[4,1,8,2,16,128]{5,4,3,2,1,0:T(8,128)(2,1)}), bf16[4,1,8,2,16,128]{5,4,3,2,1,0:T(8,128)(2,1)S(1)}, u32[]{:S(2)}, u32[]{:S(2)}) %all-to-all-start.5) | async-done | bytes 262176 | tf_op jit(solution)/shard_map/all_to_all | solution.py:467
  216.4 5.9 %all-to-all-start.4 = ((bf16[16,8,2,16,128]{4,3,2,1,0:T(8,128)(2,1)}), bf16[16,8,2,16,128]{4,3,2,1,0:T(8,128)(2,1)S(1)}, u32[]{:S(2)}, u32[]{:S(2)}) async-start(bf16[16,8,2,16,128]{4,3,2,1,0:T(8,128)(2,1)} %bitcast.8), calls=%async_computation.4 | async-start | bytes 2097152 | tf_op jit(solution)/shard_map/all_to_all | solution.py:420
  222.3 12.4 %back.2.refs_4_ = bf16[16,1024,1024]{2,1,0:T(8,128)(2,1)} custom-call(s32[1]{0:T(128)} %bitcast.where_ref, s32[1,1024]{1,0:T(1,128)} %bitcast.11, bf16[16,2,8,2,16,128]{5,4,3,2,1,0:T(8,128)(2,1)} %copy-done, bf16[16,8,2,16,128]{4,3,2,1,0:T(8,128)(2,1)} %all_to_all.30.refs_1_, bf16[16,2,8,2,16,128]{5,4,3,2,1,0:T(8,128)(2,1)} %copy-done, ...), custom_call_target="tpu_custom_call" | custom-call | flops 8589934592 | bytes 16777216 | tf_op jit(solution)/shard_map/back/pallas_call | solution.py:379
  234.8 12.4 %all-to-all-done.4.refs_1_ = bf16[16,8,2,16,128]{4,3,2,1,0:T(8,128)(2,1)S(1)} async-done(((bf16[16,8,2,16,128]{4,3,2,1,0:T(8,128)(2,1)}), bf16[16,8,2,16,128]{4,3,2,1,0:T(8,128)(2,1)S(1)}, u32[]{:S(2)}, u32[]{:S(2)}) %all-to-all-start.4) | async-done | bytes 1048608 | tf_op jit(solution)/shard_map/all_to_all | solution.py:420
  247.2 1.0 copy-done.3
  248.2 12.3 %back.3 = bf16[16,1024,1024]{2,1,0:T(8,128)(2,1)} custom-call(s32[1]{0:T(128)} %bitcast.where_ref, s32[1,1024]{1,0:T(1,128)} %bitcast.12, bf16[16,8,2,16,128]{4,3,2,1,0:T(8,128)(2,1)} %copy-done.2, bf16[16,8,2,16,128]{4,3,2,1,0:T(8,128)(2,1)} %copy-done.3, bf16[4,1,8,2,16,128]{5,4,3,2,1,0:T(8,128)(2,1)} %copy-done.4, ...), custom_call_target="tpu_custom_call", output_to_operand_aliasing={{}: (6, {})} | custom-call | flops 8589934592 | bytes 16777216 | tf_op jit(solution)/shard_map/back/pallas_call | solution.py:379
  (30 shorter events, 0.1 us)
Async XLA Ops:
  22.4 61.2 %all-to-all-start = ((bf16[16,2,8,2,16,128]{5,4,3,2,1,0:T(8,128)(2,1)}), bf16[16,2,8,2,16,128]{5,4,3,2,1,0:T(8,128)(2,1)S(1)}, u32[]{:S(2)}, u32[]{:S(2)}) async-start(bf16[16,2,8,2,16,128]{5,4,3,2,1,0:T(8,128)(2,1)} %get-tuple-element.34), calls=%async_computation | async-start | bytes 4194304 | tf_op jit(solution)/shard_map/all_to_all | solution.py:420
  29.0 52.8 %collective-permute-start.3 = (bf16[1,4,8,2,16,128]{5,4,3,2,1,0:T(8,128)(2,1)}, bf16[1,4,8,2,16,128]{5,4,3,2,1,0:T(8,128)(2,1)S(1)}, u32[]{:S(2)}, u32[]{:S(2)}) collective-permute-start(bf16[1,4,8,2,16,128]{5,4,3,2,1,0:T(8,128)(2,1)} %get-tuple-element.35.refs_0_), channel_id=1, source_target_pairs={{4,0},{5,1},{6,2},{7,3},{8,4},{9,5},{10,6},{11,7},{12,8},{13,9},{1... | collective-permute-start | bytes 786440 | tf_op jit(solution)/shard_map/ppermute | solution.py:411
  31.2 56.2 %collective-permute-start.4 = (bf16[1,4,8,2,16,128]{5,4,3,2,1,0:T(8,128)(2,1)}, bf16[1,4,8,2,16,128]{5,4,3,2,1,0:T(8,128)(2,1)S(1)}, u32[]{:S(2)}, u32[]{:S(2)}) collective-permute-start(bf16[1,4,8,2,16,128]{5,4,3,2,1,0:T(8,128)(2,1)} %get-tuple-element.36.refs_1_), channel_id=1, source_target_pairs={{8,4},{9,5},{10,6},{11,7},{12,8},{13,9},{14,10},{15,11},{24,20},{2... | collective-permute-start | bytes 786440 | tf_op jit(solution)/shard_map/ppermute | solution.py:411
  32.5 54.9 %collective-permute-start.5 = (bf16[1,4,8,2,16,128]{5,4,3,2,1,0:T(8,128)(2,1)}, bf16[1,4,8,2,16,128]{5,4,3,2,1,0:T(8,128)(2,1)S(1)}, u32[]{:S(2)}, u32[]{:S(2)}) collective-permute-start(bf16[1,4,8,2,16,128]{5,4,3,2,1,0:T(8,128)(2,1)} %get-tuple-element.37.refs_2_), channel_id=1, source_target_pairs={{12,8},{13,9},{14,10},{15,11},{28,24},{29,25},{30,26},{31,27}} | collective-permute-start | bytes 786440 | tf_op jit(solution)/shard_map/ppermute | solution.py:411
  33.1 54.2 %collective-permute-start = (bf16[1,4,8,2,16,128]{5,4,3,2,1,0:T(8,128)(2,1)}, bf16[1,4,8,2,16,128]{5,4,3,2,1,0:T(8,128)(2,1)S(1)}, u32[]{:S(2)}, u32[]{:S(2)}) collective-permute-start(bf16[1,4,8,2,16,128]{5,4,3,2,1,0:T(8,128)(2,1)} %get-tuple-element.40.refs_5_), channel_id=1, source_target_pairs={{0,4},{1,5},{2,6},{3,7},{16,20},{17,21},{18,22},{19,23}} | collective-permute-start | bytes 786440 | tf_op jit(solution)/shard_map/ppermute | solution.py:411
  34.4 52.9 %collective-permute-start.1 = (bf16[1,4,8,2,16,128]{5,4,3,2,1,0:T(8,128)(2,1)}, bf16[1,4,8,2,16,128]{5,4,3,2,1,0:T(8,128)(2,1)S(1)}, u32[]{:S(2)}, u32[]{:S(2)}) collective-permute-start(bf16[1,4,8,2,16,128]{5,4,3,2,1,0:T(8,128)(2,1)} %get-tuple-element.41.refs_6_), channel_id=1, source_target_pairs={{0,4},{1,5},{2,6},{3,7},{4,8},{5,9},{6,10},{7,11},{16,20},{17,21},... | collective-permute-start | bytes 786440 | tf_op jit(solution)/shard_map/ppermute | solution.py:411
  81.7 8.5 %copy-start.9 = (bf16[1,4,8,2,16,128]{5,4,3,2,1,0:T(8,128)(2,1)}, bf16[1,4,8,2,16,128]{5,4,3,2,1,0:T(8,128)(2,1)S(1)}, u32[]{:S(2)}) copy-start(bf16[1,4,8,2,16,128]{5,4,3,2,1,0:T(8,128)(2,1)S(1)} %collective-permute-done.3.refs_11_) | copy-start | bytes 786436
  81.7 8.5 %collective-permute-start.2 = (bf16[1,4,8,2,16,128]{5,4,3,2,1,0:T(8,128)(2,1)}, bf16[1,4,8,2,16,128]{5,4,3,2,1,0:T(8,128)(2,1)}, u32[]{:S(2)}, u32[]{:S(2)}) collective-permute-start(bf16[1,4,8,2,16,128]{5,4,3,2,1,0:T(8,128)(2,1)} %get-tuple-element.42.refs_7_), channel_id=1, source_target_pairs={{0,4},{1,5},{2,6},{3,7},{4,8},{5,9},{6,10},{7,11},{8,12},{9,13},{1... | collective-permute-start | bytes 786440 | tf_op jit(solution)/shard_map/ppermute | solution.py:411
  83.7 35.2 %copy-start = (bf16[16,2,8,2,16,128]{5,4,3,2,1,0:T(8,128)(2,1)}, bf16[16,2,8,2,16,128]{5,4,3,2,1,0:T(8,128)(2,1)S(1)}, u32[]{:S(2)}) copy-start(bf16[16,2,8,2,16,128]{5,4,3,2,1,0:T(8,128)(2,1)S(1)} %all-to-all-done.refs_0_.refs_2_) | copy-start | bytes 6291460
  87.4 2.9 %copy-start.10 = (bf16[1,4,8,2,16,128]{5,4,3,2,1,0:T(8,128)(2,1)}, bf16[1,4,8,2,16,128]{5,4,3,2,1,0:T(8,128)(2,1)S(1)}, u32[]{:S(2)}) copy-start(bf16[1,4,8,2,16,128]{5,4,3,2,1,0:T(8,128)(2,1)S(1)} %collective-permute-done.4.refs_12_) | copy-start | bytes 786436
  87.4 2.9 %copy-start.11 = (bf16[1,4,8,2,16,128]{5,4,3,2,1,0:T(8,128)(2,1)}, bf16[1,4,8,2,16,128]{5,4,3,2,1,0:T(8,128)(2,1)S(1)}, u32[]{:S(2)}) copy-start(bf16[1,4,8,2,16,128]{5,4,3,2,1,0:T(8,128)(2,1)S(1)} %collective-permute-done.5.refs_13_) | copy-start | bytes 786436
  87.4 2.9 %copy-start.12 = (bf16[1,4,8,2,16,128]{5,4,3,2,1,0:T(8,128)(2,1)}, bf16[1,4,8,2,16,128]{5,4,3,2,1,0:T(8,128)(2,1)S(1)}, u32[]{:S(2)}) copy-start(bf16[1,4,8,2,16,128]{5,4,3,2,1,0:T(8,128)(2,1)S(1)} %collective-permute-done.refs_8_) | copy-start | bytes 786436
  87.4 2.9 %copy-start.13 = (bf16[1,4,8,2,16,128]{5,4,3,2,1,0:T(8,128)(2,1)}, bf16[1,4,8,2,16,128]{5,4,3,2,1,0:T(8,128)(2,1)S(1)}, u32[]{:S(2)}) copy-start(bf16[1,4,8,2,16,128]{5,4,3,2,1,0:T(8,128)(2,1)S(1)} %collective-permute-done.1.refs_9_) | copy-start | bytes 786436
  94.4 44.0 %all-to-all-start.1 = ((bf16[16,8,2,16,128]{4,3,2,1,0:T(8,128)(2,1)}), bf16[16,8,2,16,128]{4,3,2,1,0:T(8,128)(2,1)S(1)}, u32[]{:S(2)}, u32[]{:S(2)}) async-start(bf16[16,8,2,16,128]{4,3,2,1,0:T(8,128)(2,1)} %bitcast.7), calls=%async_computation.1 | async-start | bytes 2097152 | tf_op jit(solution)/shard_map/all_to_all | solution.py:420
  118.8 17.6 %collective-permute-start.9 = (bf16[2,4,8,2,16,128]{5,4,3,2,1,0:T(8,128)(2,1)}, bf16[2,4,8,2,16,128]{5,4,3,2,1,0:T(8,128)(2,1)S(1)}, u32[]{:S(2)}, u32[]{:S(2)}) collective-permute-start(bf16[2,4,8,2,16,128]{5,4,3,2,1,0:T(8,128)(2,1)} %get-tuple-element.46.refs_0_), channel_id=1, source_target_pairs={{4,0},{5,1},{6,2},{7,3},{8,4},{9,5},{10,6},{11,7},{12,8},{13,9},{1... | collective-permute-start | bytes 1572872 | tf_op jit(solution)/shard_map/ppermute | solution.py:411
  121.0 26.7 %collective-permute-start.10 = (bf16[2,4,8,2,16,128]{5,4,3,2,1,0:T(8,128)(2,1)}, bf16[2,4,8,2,16,128]{5,4,3,2,1,0:T(8,128)(2,1)S(1)}, u32[]{:S(2)}, u32[]{:S(2)}) collective-permute-start(bf16[2,4,8,2,16,128]{5,4,3,2,1,0:T(8,128)(2,1)} %get-tuple-element.47.refs_1_), channel_id=1, source_target_pairs={{8,4},{9,5},{10,6},{11,7},{12,8},{13,9},{14,10},{15,11},{24,20},{2... | collective-permute-start | bytes 1572872 | tf_op jit(solution)/shard_map/ppermute | solution.py:411
  122.3 25.5 %collective-permute-start.11 = (bf16[2,4,8,2,16,128]{5,4,3,2,1,0:T(8,128)(2,1)}, bf16[2,4,8,2,16,128]{5,4,3,2,1,0:T(8,128)(2,1)S(1)}, u32[]{:S(2)}, u32[]{:S(2)}) collective-permute-start(bf16[2,4,8,2,16,128]{5,4,3,2,1,0:T(8,128)(2,1)} %get-tuple-element.48.refs_2_), channel_id=1, source_target_pairs={{12,8},{13,9},{14,10},{15,11},{28,24},{29,25},{30,26},{31,27}} | collective-permute-start | bytes 1572872 | tf_op jit(solution)/shard_map/ppermute | solution.py:411
  123.0 24.8 %collective-permute-start.6 = (bf16[2,4,8,2,16,128]{5,4,3,2,1,0:T(8,128)(2,1)}, bf16[2,4,8,2,16,128]{5,4,3,2,1,0:T(8,128)(2,1)S(1)}, u32[]{:S(2)}, u32[]{:S(2)}) collective-permute-start(bf16[2,4,8,2,16,128]{5,4,3,2,1,0:T(8,128)(2,1)} %get-tuple-element.51.refs_5_), channel_id=1, source_target_pairs={{0,4},{1,5},{2,6},{3,7},{16,20},{17,21},{18,22},{19,23}} | collective-permute-start | bytes 1572872 | tf_op jit(solution)/shard_map/ppermute | solution.py:411
  124.3 24.9 %collective-permute-start.7 = (bf16[2,4,8,2,16,128]{5,4,3,2,1,0:T(8,128)(2,1)}, bf16[2,4,8,2,16,128]{5,4,3,2,1,0:T(8,128)(2,1)}, u32[]{:S(2)}, u32[]{:S(2)}) collective-permute-start(bf16[2,4,8,2,16,128]{5,4,3,2,1,0:T(8,128)(2,1)} %get-tuple-element.52.refs_6_), channel_id=1, source_target_pairs={{0,4},{1,5},{2,6},{3,7},{4,8},{5,9},{6,10},{7,11},{16,20},{17,21},... | collective-permute-start | bytes 1572872 | tf_op jit(solution)/shard_map/ppermute | solution.py:411
  136.4 24.1 %copy-start.5 = (bf16[2,4,8,2,16,128]{5,4,3,2,1,0:T(8,128)(2,1)}, bf16[2,4,8,2,16,128]{5,4,3,2,1,0:T(8,128)(2,1)S(1)}, u32[]{:S(2)}) copy-start(bf16[2,4,8,2,16,128]{5,4,3,2,1,0:T(8,128)(2,1)S(1)} %collective-permute-done.9.refs_11_) | copy-start | bytes 1572868
  136.4 24.1 %collective-permute-start.8 = (bf16[2,4,8,2,16,128]{5,4,3,2,1,0:T(8,128)(2,1)}, bf16[2,4,8,2,16,128]{5,4,3,2,1,0:T(8,128)(2,1)}, u32[]{:S(2)}, u32[]{:S(2)}) collective-permute-start(bf16[2,4,8,2,16,128]{5,4,3,2,1,0:T(8,128)(2,1)} %get-tuple-element.53.refs_7_), channel_id=1, source_target_pairs={{0,4},{1,5},{2,6},{3,7},{4,8},{5,9},{6,10},{7,11},{8,12},{9,13},{1... | collective-permute-start | bytes 1572872 | tf_op jit(solution)/shard_map/ppermute | solution.py:411
  138.4 96.4 %copy-start.2 = (bf16[16,8,2,16,128]{4,3,2,1,0:T(8,128)(2,1)}, bf16[16,8,2,16,128]{4,3,2,1,0:T(8,128)(2,1)S(1)}, u32[]{:S(2)}) copy-start(bf16[16,8,2,16,128]{4,3,2,1,0:T(8,128)(2,1)S(1)} %all-to-all-done.1.refs_0_) | copy-start | bytes 3145732
  147.8 12.7 %copy-start.6 = (bf16[2,4,8,2,16,128]{5,4,3,2,1,0:T(8,128)(2,1)}, bf16[2,4,8,2,16,128]{5,4,3,2,1,0:T(8,128)(2,1)S(1)}, u32[]{:S(2)}) copy-start(bf16[2,4,8,2,16,128]{5,4,3,2,1,0:T(8,128)(2,1)S(1)} %collective-permute-done.10.refs_12_) | copy-start | bytes 1572868
  147.8 12.7 %copy-start.7 = (bf16[2,4,8,2,16,128]{5,4,3,2,1,0:T(8,128)(2,1)}, bf16[2,4,8,2,16,128]{5,4,3,2,1,0:T(8,128)(2,1)S(1)}, u32[]{:S(2)}) copy-start(bf16[2,4,8,2,16,128]{5,4,3,2,1,0:T(8,128)(2,1)S(1)} %collective-permute-done.11.refs_13_) | copy-start | bytes 1572868
  147.8 12.7 %copy-start.8 = (bf16[2,4,8,2,16,128]{5,4,3,2,1,0:T(8,128)(2,1)}, bf16[2,4,8,2,16,128]{5,4,3,2,1,0:T(8,128)(2,1)S(1)}, u32[]{:S(2)}) copy-start(bf16[2,4,8,2,16,128]{5,4,3,2,1,0:T(8,128)(2,1)S(1)} %collective-permute-done.6.refs_8_) | copy-start | bytes 1572868
  196.2 11.3 %all-to-all-start.3 = ((bf16[4,2,8,2,16,128]{5,4,3,2,1,0:T(8,128)(2,1)}), bf16[4,2,8,2,16,128]{5,4,3,2,1,0:T(8,128)(2,1)S(1)}, u32[]{:S(2)}, u32[]{:S(2)}) async-start(bf16[4,2,8,2,16,128]{5,4,3,2,1,0:T(8,128)(2,1)} %get-tuple-element.57), calls=%async_computation.3 | async-start | bytes 1048576 | tf_op jit(solution)/shard_map/all_to_all | solution.py:467
  207.4 14.9 %copy-start.1 = (bf16[4,2,8,2,16,128]{5,4,3,2,1,0:T(8,128)(2,1)}, bf16[4,2,8,2,16,128]{5,4,3,2,1,0:T(8,128)(2,1)S(1)}, u32[]{:S(2)}) copy-start(bf16[4,2,8,2,16,128]{5,4,3,2,1,0:T(8,128)(2,1)S(1)} %all-to-all-done.3.refs_3_) | copy-start | bytes 1572868
  207.4 9.0 %all-to-all-start.5 = ((bf16[4,1,8,2,16,128]{5,4,3,2,1,0:T(8,128)(2,1)}), bf16[4,1,8,2,16,128]{5,4,3,2,1,0:T(8,128)(2,1)S(1)}, u32[]{:S(2)}, u32[]{:S(2)}) async-start(bf16[4,1,8,2,16,128]{5,4,3,2,1,0:T(8,128)(2,1)} %get-tuple-element.60), calls=%async_computation.5 | async-start | bytes 524288 | tf_op jit(solution)/shard_map/all_to_all | solution.py:467
  216.4 18.3 %copy-start.4 = (bf16[4,1,8,2,16,128]{5,4,3,2,1,0:T(8,128)(2,1)}, bf16[4,1,8,2,16,128]{5,4,3,2,1,0:T(8,128)(2,1)S(1)}, u32[]{:S(2)}) copy-start(bf16[4,1,8,2,16,128]{5,4,3,2,1,0:T(8,128)(2,1)S(1)} %all-to-all-done.5.refs_2_) | copy-start | bytes 786436
  216.4 30.7 %all-to-all-start.4 = ((bf16[16,8,2,16,128]{4,3,2,1,0:T(8,128)(2,1)}), bf16[16,8,2,16,128]{4,3,2,1,0:T(8,128)(2,1)S(1)}, u32[]{:S(2)}, u32[]{:S(2)}) async-start(bf16[16,8,2,16,128]{4,3,2,1,0:T(8,128)(2,1)} %bitcast.8), calls=%async_computation.4 | async-start | bytes 2097152 | tf_op jit(solution)/shard_map/all_to_all | solution.py:420
  247.2 1.0 copy-start.3

commit v4 on v3

--- a/solution.py
+++ b/solution.py
@@ -21,9 +21,8 @@
         return phase_index.astype(jnp.float32) * (2.0 * math.pi / frame_len)
 
     fine = angles(jnp.arange(LANES, dtype=jnp.int32))
-    coarse = angles(jnp.arange(0, frame_len, LANES, dtype=jnp.int32)).T[:, :, None]
-    fine = jnp.stack([jnp.cos(fine) * norm_scale, jnp.sin(fine) * norm_scale])
-    return fine, jnp.stack([jnp.cos(coarse), jnp.sin(coarse)], axis=1)
+    coarse = angles(jnp.arange(0, frame_len, LANES, dtype=jnp.int32)).T
+    return jnp.cos(fine) * norm_scale, jnp.sin(fine) * norm_scale, jnp.cos(coarse), jnp.sin(coarse)
 
 
 def tap_leaves(taps):
@@ -61,7 +60,7 @@
     return outs + high[half - 1 :]
 
 
-def front_kernel(groups, x_ref, fir_ref, fine_ref, coarse_ref, *rest):
+def front_kernel(groups, x_ref, fir_ref, cos_ref, sin_ref, cos_turn, sin_turn, *rest):
     outs, (filt, table, coeffs, spread) = rest[:-4], rest[-4:]
     sets = sum(len(members) for members, _ in groups)
     frames, slots, lanes = x_ref.shape
@@ -70,16 +69,14 @@
     columns = pl.ds(pl.multiple_of(step * lanes, lanes), lanes)
     recursive = taps == frames and frames & (frames - 1) == 0
 
-    chans = fine_ref.shape[1]
-    turn = [coarse_ref[0, part] for part in range(2)]
-    held = chans // sets
-    rows = [fine_ref[0] * turn[0] - fine_ref[1] * turn[1]]
-    rows += [-(fine_ref[1] * turn[0] + fine_ref[0] * turn[1])]
-    for each in range(sets):
-        for part in range(2):
-            first = (each * 2 + part) * held
-            piece = rows[part][each * held : (each + 1) * held]
-            table[first : first + held, columns] = piece.astype(jnp.bfloat16)
+    chans = cos_ref.shape[0]
+    turns = [
+        jnp.broadcast_to(turn[pl.ds(step, 1), :], (lanes, chans)).T for turn in (cos_turn, sin_turn)
+    ]
+    real = cos_ref[...] * turns[0] - sin_ref[...] * turns[1]
+    imag = -(sin_ref[...] * turns[0] + cos_ref[...] * turns[1])
+    table[:chans, columns] = real.astype(jnp.bfloat16)
+    table[chans:, columns] = imag.astype(jnp.bfloat16)
 
     leaves = [fir_ref[tap : tap + 1, :] for tap in range(taps)]
     leaves = tap_leaves(leaves) if recursive else [leaves]
@@ -110,22 +107,22 @@
 
     lax.fori_loop(0, slots // 16, filter_rows, 0)
 
-    def deliver(part, each, which, values):
+    def deliver(part, which, values):
         first = 0
         for members, whole in groups:
             refs = outs[first : first + (1 if whole else 2 * QUART)]
             first += len(refs)
-            if each not in members:
-                continue
-            if whole:
-                dests, _, per_dest = refs[0].shape[:3]
-                refs[0][:, part, :, which] = values.reshape(dests, per_dest, frames, slots)
-            else:
-                _, plane, per_dest = refs[0].shape[:3]
-                values = values.reshape(QUART, plane, per_dest, frames, slots)
+            per_dest = refs[0].shape[2]
+            shaped = values.reshape(-1, sets, per_dest, frames, slots)
+            for index, each in enumerate(members):
+                mine = shaped[:, each].astype(jnp.bfloat16)
+                if whole:
+                    refs[0][:, part, :, which] = mine
+                    continue
+                plane = mine.shape[0] // QUART
                 for target in range(QUART):
                     out = refs[part * QUART + target]
-                    out[members.index(each), :, :, which] = values[target]
+                    out[index, :, :, which] = mine[target * plane : (target + 1) * plane]
 
     @pl.when(step == pl.num_programs(0) - 1)
     def _():
@@ -139,9 +136,8 @@
                     preferred_element_type=jnp.float32,
                 )
                 result = result.reshape(-1, frames, slots)
-                for piece in range(2 * sets):
-                    values = result[piece * held : (piece + 1) * held].astype(jnp.bfloat16)
-                    deliver(part, piece // 2, piece % 2, values)
+                for which in range(2):
+                    deliver(part, which, result[which * chans : (which + 1) * chans])
             else:
 
                 def transform(frame, carry):
@@ -155,17 +151,16 @@
                     return carry
 
                 lax.fori_loop(0, frames, transform, 0)
-                for piece in range(2 * sets):
-                    values = spread[piece * held * frames : (piece + 1) * held * frames, :]
-                    values = values.astype(jnp.bfloat16).reshape(held, frames, slots)
-                    deliver(part, piece // 2, piece % 2, values)
-
-
-def front(x, fir, fine, coarse, block, blocks, groups, dests):
+                for which in range(2):
+                    values = spread[which * chans * frames : (which + 1) * chans * frames, :]
+                    deliver(part, which, values.reshape(chans, frames, slots))
+
+
+def front(x, fir, angles, block, blocks, groups, dests):
     frames, slots_dev, frame_len = x.shape
     slots = slots_dev // blocks
     taps = fir.shape[0]
-    chans = fine.shape[1]
+    chans = angles[0].shape[0]
     sets = sum(len(members) for members, _ in groups)
     tail = (chans // sets // dests, 2, frames, slots)
     shapes = []
@@ -181,8 +176,10 @@
         in_specs=[
             pl.BlockSpec((frames, slots, LANES), lambda j: (0, block, j)),
             pl.BlockSpec((taps, LANES), lambda j: (0, j)),
-            pl.BlockSpec(fine.shape, lambda j: (0, 0, 0), pipeline_mode=pl.Buffered(1)),
-            pl.BlockSpec((1, 2, chans, 1), lambda j: (j, 0, 0, 0)),
+        ]
+        + [
+            pl.BlockSpec(angle.shape, lambda j: (0, 0), pipeline_mode=pl.Buffered(1))
+            for angle in angles
         ],
         out_specs=[
             pl.BlockSpec(shape, lambda j: (0, 0, 0, 0, 0, 0), pipeline_mode=pl.Buffered(1))
@@ -201,14 +198,16 @@
             transcendentals=0,
         ),
         name="front",
-    )(x, fir, fine, coarse)
+    )(x, fir, *angles)
 
 
 def meet_kernel(sets, where_ref, *refs):
     owns, lates = refs[:QUART], refs[QUART : 2 * QUART]
     risen, fallen = refs[2 * QUART : 3 * QUART - 1], refs[3 * QUART - 1 : 4 * QUART - 2]
-    outs, side = refs[4 * QUART - 2 : -1], refs[-1]
+    outs, sides, hold = refs[4 * QUART - 2 :][:sets], refs[4 * QUART - 2 :][sets:-1], refs[-1]
     here = where_ref[0]
+    offset = pl.program_id(0) - where_ref[1]
+    offset = jnp.where(offset < 0, offset + len(sides), offset)
 
     def add(one, other):
         return (one.astype(jnp.float32) + other.astype(jnp.float32)).astype(jnp.bfloat16)
@@ -232,19 +231,25 @@
         @pl.when(here == target)
         def _():
             for each in range(sets):
-                side[0, each] = add(fallen[target][each, 0], lates[target][each, 0])
+                hold[each] = add(fallen[target][each, 0], lates[target][each, 0])
 
     @pl.when(here == QUART - 1)
     def _():
-        side[...] = jnp.zeros_like(side)
-
-
-def meet(quarter, owns, lates, risen, fallen):
+        hold[...] = jnp.zeros_like(hold)
+
+    for distance, side in enumerate(sides):
+
+        @pl.when(offset == distance)
+        def _():
+            side[...] = hold[...]
+
+
+def meet(where, owns, lates, risen, fallen):
     sets, plane, *tail = owns[0].shape
     block = pl.BlockSpec((sets, 1, *tail), lambda g, _: (0, g, 0, 0, 0, 0))
     out = pl.BlockSpec((QUART, 1, *tail), lambda g, _: (0, g, 0, 0, 0, 0))
-    side = pl.BlockSpec((1, sets, *tail), lambda g, _: (g, 0, 0, 0, 0, 0))
-    shapes = [(QUART, plane, *tail)] * sets + [(plane, sets, *tail)]
+    side = pl.BlockSpec((sets, *tail), lambda g, _: (0, 0, 0, 0, 0))
+    shapes = [(QUART, plane, *tail)] * sets + [(sets, *tail)] * plane
     operands = [*owns, *lates, *risen, *fallen]
     return pl.pallas_call(
         functools.partial(meet_kernel, sets),
@@ -252,18 +257,23 @@
             num_scalar_prefetch=1,
             grid=(plane,),
             in_specs=[block] * len(operands),
-            out_specs=[out] * sets + [side],
+            out_specs=[out] * sets + [side] * plane,
+            scratch_shapes=[pltpu.VMEM((sets, *tail), jnp.bfloat16)],
         ),
         out_shape=[jax.ShapeDtypeStruct(shape, jnp.bfloat16) for shape in shapes],
         cost_estimate=pl.CostEstimate(
             flops=sets * owns[0].size * 5, bytes_accessed=owns[0].size * 40, transcendentals=0
         ),
         name="meet",
-    )(quarter, *operands)
+    )(where, *operands)
 
 
 def back_kernel(kinds, groups, pair, scale, where_ref, order_ref, *refs):
-    firsts, seconds = refs[: len(kinds)], refs[len(kinds) : 2 * len(kinds)]
+    firsts, seconds, used = refs[: len(kinds)], [], len(kinds)
+    for kind in kinds:
+        count = 1 if kind == "whole" else groups
+        seconds.append(refs[used : used + count])
+        used += count
     out_ref, pick, ordered, turned = refs[-4:]
     inputs = out_ref.shape[-1]
     tile = min(256, inputs)
@@ -276,7 +286,7 @@
             hit = jnp.where(order_ref[...] == wanted, 1.0, 0.0)
             pick[first : first + tile, :] = hit.astype(jnp.bfloat16)
 
-    def rows_of(kind, first, second, group, place, chan, part):
+    def rows_of(kind, first, second, distance, group, place, chan, part):
         if kind == "whole":
             if place == 0:
                 return first[group, 0, chan, part]
@@ -284,21 +294,24 @@
             if place == QUART - 1:
                 quarter = jnp.minimum(here + 1, QUART - 1)
             own = first[quarter * groups + group, 0, chan, part].astype(jnp.float32)
-            before = second[(quarter - 1) * groups + group, 0, chan, part].astype(jnp.float32)
+            before = second[0][(quarter - 1) * groups + group, 0, chan, part].astype(jnp.float32)
             return (own + before).astype(jnp.bfloat16)
         value = first[place * groups + group, chan, part]
         if place == QUART - 1:
-            value = jnp.where(here < QUART - 1, second[group, 0, chan, part], value)
+            value = jnp.where(here < QUART - 1, second[distance][0, chan, part], value)
         return value
 
     pieces = []
-    for group in range(groups):
+    for distance in range(groups):
+        group = where_ref[1] - distance
+        group = jnp.where(group < 0, group + groups, group)
         for kind, first, second in zip(kinds, firsts, seconds):
             rows = []
             for chan in range(pair):
                 for part in range(2):
                     for place in range(QUART):
-                        rows.append(rows_of(kind, first, second, group, place, chan, part))
+                        row = rows_of(kind, first, second, distance, group, place, chan, part)
+                        rows.append(row)
             pieces.append(jnp.concatenate(rows, axis=0))
     stacked = jnp.concatenate(pieces, axis=1)
     depth = stacked.shape[0] // pair
@@ -340,7 +353,7 @@
                 out_ref[chan, first : first + tile, place] = (result * scale).astype(jnp.bfloat16)
 
 
-def back(quarter, order, datas, each, sets, chan_dev, earlier):
+def back(where, order, datas, each, sets, chan_dev, earlier):
     inputs = order.shape[1]
     held = chan_dev // sets
     pair = 2 if held % 2 == 0 else 1
@@ -359,15 +372,13 @@
                     pl.BlockSpec((sources, 1, *tail), lambda k, _, part=part: (0, part, k, 0, 0, 0))
                 )
         else:
-            seconds.append(arrays[1])
+            seconds += arrays[1]
             member = arrays[2]
             first_specs.append(pl.BlockSpec((sources, *tail), lambda k, _: (0, k, 0, 0, 0)))
-            second_specs.append(
-                pl.BlockSpec(
-                    (groups, 1, *tail), lambda k, _, member=member: (0, member, k, 0, 0, 0)
-                )
-            )
-    operands = [quarter, order, *firsts, *seconds]
+            second_specs += [
+                pl.BlockSpec((1, *tail), lambda k, _, member=member: (member, k, 0, 0, 0))
+            ] * groups
+    operands = [where, order, *firsts, *seconds]
     in_specs = [pl.BlockSpec((1, inputs), lambda k, _: (0, 0)), *first_specs, *second_specs]
     aliases = {}
     scale = 1.0 / (QUART * frames)
@@ -416,6 +427,14 @@
     return lax.optimization_barrier((value, earlier))[0]
 
 
+def mark(value):
+    def kernel(value_ref, out_ref):
+        out_ref[...] = value_ref[...]
+
+    shape = jax.ShapeDtypeStruct(value.shape, value.dtype)
+    return pl.pallas_call(kernel, out_shape=shape, name="mark")(value)
+
+
 def exchange(value):
     return lax.all_to_all(value, "chan", split_axis=0, concat_axis=0, tiled=True)
 
@@ -427,13 +446,12 @@
     plane = chan_count // QUART
     chan_dev = chan_assign.shape[0] // chan_count
     sets = 2 if chan_dev % 2 == 0 else 1
-    held = chan_dev // sets
     blocks = 2 if slots_dev % (2 * LANES) == 0 else 1
-    chans = chan_assign.reshape(chan_count, sets, held).transpose(1, 0, 2).reshape(-1)
-    fine, coarse = split_table(chans, frame_len)
-    order = input_order[None, :]
-    quarter = (lax.axis_index("chan") // plane).astype(jnp.int32)[None]
-    planes = [[q * plane + i for i in range(plane)] for q in range(QUART)]
+    angles = split_table(chan_assign, frame_len)
+    here = lax.axis_index("chan").astype(jnp.int32)
+    where = jnp.stack([here // plane, here % plane])
+    order = jnp.concatenate([input_order, input_order]).reshape(2 * plane, -1)[::-1]
+    order = lax.dynamic_slice_in_dim(order, plane - 1 - here % plane, plane).reshape(1, -1)
 
     ready = [[None] * blocks for _ in range(sets)]
     source, token, pending = own_frames, None, []
@@ -442,7 +460,7 @@
             groups = [((0,), True)] + [((each,), False) for each in range(1, sets)]
         else:
             groups = [(tuple(range(sets)), False)]
-        parts = front(source, fir, fine, coarse, block, blocks, groups, chan_count)
+        parts = front(source, fir, angles, block, blocks, groups, chan_count)
         source = after(own_frames, parts[0])
         for members, whole in groups:
             if whole:
@@ -455,28 +473,27 @@
             fallen = hops(list(enumerate(owns))[:-1], plane, False)
             pending.append((block, members, owns, lates, risen, fallen))
     for block, members, owns, lates, risen, fallen in pending:
-        *met, side = meet(quarter, [after(owns[0], token), *owns[1:]], lates, risen, fallen)
-        swapped = []
-        for index in range(len(members)):
+        owns = [after(owns[0], token), *owns[1:]]
+        met = meet(where, owns, lates, risen, fallen)
+        met, sides = met[: len(members)], list(met[len(members) :])
+        for distance in range(1, plane):
+            moves = [
+                (q * plane + i, q * plane + (i + distance) % plane)
+                for q in range(QUART)
+                for i in range(plane)
+            ]
+            sides[distance] = lax.ppermute(sides[distance], "chan", moves)
+        for index, each in enumerate(members):
             block_met = met[index].reshape(chan_count, *met[index].shape[2:])
             if index:
-                block_met = after(block_met, side)
+                block_met = after(block_met, token)
             token = exchange(block_met)
-            swapped.append(token)
-            if index == 0:
-                side = lax.all_to_all(
-                    after(side, token),
-                    "chan",
-                    split_axis=0,
-                    concat_axis=0,
-                    axis_index_groups=planes,
-                    tiled=True,
-                )
-        for index, each in enumerate(members):
-            ready[each][block] = ("met", swapped[index], side, index)
+            ready[each][block] = ("met", token, sides, index)
+    for _ in range(2):
+        order = mark(order)
     vis = None
     for each in range(sets):
-        vis = back(quarter, order, ready[each], each, sets, chan_dev, vis)
+        vis = back(where, order, ready[each], each, sets, chan_dev, vis)
     return vis
 
 

time: 262 us -> 249 us (0.950); the launches traced: 260 us -> 245 us
  waiting for transfers between devices: 104 us -> 84.9 us
  Pallas kernels: 70.5 us -> 75.8 us
  starting transfers between devices: 50.1 us -> 46.8 us
  other arithmetic: 1.45 us -> 4.08 us
    all_to_all x3, waiting for transfers between devices: 12.4 us -> 0.01 us  [exchange(): lax.all_to_all(value, 'chan', split_axis=0, concat_axis=0, tiled=True)]
    all_to_all x2 -> x0, waiting for transfers between devices: 11.5 us -> none  [on_device(): lax.all_to_all(after(side, token), 'chan', split_axis=0, concat_axis=0, a...]
    all_to_all x2 -> x0, starting transfers between devices: 8.77 us -> none  [on_device(): lax.all_to_all(after(side, token), 'chan', split_axis=0, concat_axis=0, a...]
    ppermute x0 -> x6, starting transfers between devices: none -> 6.26 us  [on_device(): sides[distance] = lax.ppermute(sides[distance], 'chan', moves)]
    ppermute x0 -> x6, waiting for transfers between devices: none -> 5.51 us  [on_device(): sides[distance] = lax.ppermute(sides[distance], 'chan', moves)]
  transfers between devices with their start and end apart: 17 -> 21, of which waited for: 10 -> 10; matrix products, arithmetic and copies ran while one was open for 0% -> 1% of each run, Pallas kernels for 12% -> 14%
where the time goes in v4:
time: 249 us; the launch traced here: 245 us
  waiting for transfers between devices  84.9 us (34%)
  Pallas kernels  75.8 us (30%)
  starting transfers between devices  46.8 us (19%)
  blocking collectives  30.3 us (12%)
  other arithmetic  4.08 us (2%)
    ppermute x12, waiting for transfers between devices, hops(): lax.ppermute(value, 'chan', [(place, place + step) for place in places])  79.4 us
    pallas_call x2, Pallas kernels, front(): pl.pallas_call(functools.partial(front_kernel, groups), grid=(frame_len /...  36.1 us
    all_to_all x1, blocking collectives, exchange(): lax.all_to_all(value, 'chan', split_axis=0, concat_axis=0, tiled=True)  30.3 us
    pallas_call x2, Pallas kernels, back(): pl.pallas_call(functools.partial(back_kernel, kinds, groups, pair, scale)...  26.2 us
    ppermute x12, starting transfers between devices, hops(): lax.ppermute(value, 'chan', [(place, place + step) for place in places])  22.8 us
    all_to_all x3, starting transfers between devices, exchange(): lax.all_to_all(value, 'chan', split_axis=0, concat_axis=0, tiled=True)  17.7 us
    pallas_call x2, Pallas kernels, meet(): pl.pallas_call(functools.partial(meet_kernel, sets), grid_spec=pltpu.Pref...  10.9 us
    ppermute x6, starting transfers between devices, on_device(): sides[distance] = lax.ppermute(sides[distance], 'chan', moves)  6.26 us
  transfers between devices with their start and end apart: 21, of which 10 were waited for; matrix products, arithmetic and copies ran while one was open for 1% of the time, Pallas kernels for 14%

profile of v4, /device:TPU:13, one launch (start us, length us, event | category | flops | bytes accessed | tf_op | source)
XLA Modules:
  0.0 244.6 jit_solution(1537882110038180152)
XLA Ops:
  0.0 2.0 sine_multiply_fusion
  2.0 1.4 fusion.9
  3.4 18.1 %front.2 = (bf16[16,2,8,2,16,128]{5,4,3,2,1,0:T(8,128)(2,1)}, bf16[1,4,8,2,16,128]{5,4,3,2,1,0:T(8,128)(2,1)}, bf16[1,4,8,2,16,128]{5,4,3,2,1,0:T(8,128)(2,1)}, ...) custom-call(bf16[16,256,1024]{2,1,0:T(8,128)(2,1)} %bitcast.14, ...), custom_call_target="tpu_custom_call" | custom-call | flops 4294967296 | bytes 8388608 | tf_op jit(solution)/shard_map/front/pallas_call | solution.py:173
  21.5 6.5 %all-to-all-start = ((bf16[16,2,8,2,16,128]{5,4,3,2,1,0:T(8,128)(2,1)}), bf16[16,2,8,2,16,128]{5,4,3,2,1,0:T(8,128)(2,1)S(1)}, u32[]{:S(2)}, u32[]{:S(2)}) async-start(bf16[16,2,8,2,16,128]{5,4,3,2,1,0:T(8,128)(2,1)} %get-tuple-element.38), calls=%async_computation | async-start | bytes 4194304 | tf_op jit(solution)/shard_map/all_to_all | solution.py:439
  28.0 2.2 collective-permute-start.3
  30.2 1.3 collective-permute-start.4
  31.5 0.7 collective-permute-start.5
  32.2 1.3 collective-permute-start
  33.5 4.0 %collective-permute-start.1 = (bf16[1,4,8,2,16,128]{5,4,3,2,1,0:T(8,128)(2,1)}, bf16[1,4,8,2,16,128]{5,4,3,2,1,0:T(8,128)(2,1)S(1)}, u32[]{:S(2)}, u32[]{:S(2)}) collective-permute-start(bf16[1,4,8,2,16,128]{5,4,3,2,1,0:T(8,128)(2,1)} %get-tuple-element.45.refs_6_), channel_id=1, source_target_pairs={{0,4},{1,5},{2,6},{3,7},{4,8},{5,9},{6,10},{7,11},{16,20},{17,21},... | collective-permute-start | bytes 786440 | tf_op jit(solution)/shard_map/ppermute | solution.py:422
  37.5 43.3 %collective-permute-done.3.refs_11_ = bf16[1,4,8,2,16,128]{5,4,3,2,1,0:T(8,128)(2,1)S(1)} collective-permute-done((bf16[1,4,8,2,16,128]{5,4,3,2,1,0:T(8,128)(2,1)}, bf16[1,4,8,2,16,128]{5,4,3,2,1,0:T(8,128)(2,1)S(1)}, u32[]{:S(2)}, u32[]{:S(2)}) %collective-permute-start.3) | collective-permute-done | bytes 262176 | tf_op jit(solution)/shard_map/ppermute | solution.py:422
  80.8 1.9 collective-permute-start.2
  82.7 0.7 pad_add_fusion.1.where_ref
  83.4 3.0 %collective-permute-done.4.refs_12_ = bf16[1,4,8,2,16,128]{5,4,3,2,1,0:T(8,128)(2,1)S(1)} collective-permute-done((bf16[1,4,8,2,16,128]{5,4,3,2,1,0:T(8,128)(2,1)}, bf16[1,4,8,2,16,128]{5,4,3,2,1,0:T(8,128)(2,1)S(1)}, u32[]{:S(2)}, u32[]{:S(2)}) %collective-permute-start.4) | collective-permute-done | bytes 262176 | tf_op jit(solution)/shard_map/ppermute | solution.py:422
  86.4 2.9 %collective-permute-done.2.refs_10_ = bf16[1,4,8,2,16,128]{5,4,3,2,1,0:T(8,128)(2,1)} collective-permute-done((bf16[1,4,8,2,16,128]{5,4,3,2,1,0:T(8,128)(2,1)}, bf16[1,4,8,2,16,128]{5,4,3,2,1,0:T(8,128)(2,1)}, u32[]{:S(2)}, u32[]{:S(2)}) %collective-permute-start.2) | collective-permute-done | bytes 262176 | tf_op jit(solution)/shard_map/ppermute | solution.py:422
  89.3 4.8 %meet.2 = (bf16[4,4,8,2,16,128]{5,4,3,2,1,0:T(8,128)(2,1)}, bf16[1,8,2,16,128]{4,3,2,1,0:T(8,128)(2,1)}, bf16[1,8,2,16,128]{4,3,2,1,0:T(8,128)(2,1)}, bf16[1,8,2...) custom-call(s32[2]{0:T(128)} %pad_add_fusion.1.where_ref, bf16[1,4,8,2,16,128]{5,4,3,2,1,0:T(8,128)(2,1)} %get-tuple-element.39.refs_0_, ...), custom_call_target="tpu_custom_call" | custom-call | flops 655360 | bytes 5242880 | tf_op jit(solution)/shard_map/meet/pallas_call | solution.py:254
  94.1 6.2 %all-to-all-start.1 = ((bf16[16,8,2,16,128]{4,3,2,1,0:T(8,128)(2,1)}), bf16[16,8,2,16,128]{4,3,2,1,0:T(8,128)(2,1)S(1)}, u32[]{:S(2)}, u32[]{:S(2)}) async-start(bf16[16,8,2,16,128]{4,3,2,1,0:T(8,128)(2,1)} %bitcast.11), calls=%async_computation.1 | async-start | bytes 2097152 | tf_op jit(solution)/shard_map/all_to_all | solution.py:439
  100.4 18.0 %front.3 = (bf16[2,4,8,2,16,128]{5,4,3,2,1,0:T(8,128)(2,1)}, bf16[2,4,8,2,16,128]{5,4,3,2,1,0:T(8,128)(2,1)}, bf16[2,4,8,2,16,128]{5,4,3,2,1,0:T(8,128)(2,1)}, b...) custom-call(bf16[16,256,1024]{2,1,0:T(8,128)(2,1)} %bitcast.15, ...), custom_call_target="tpu_custom_call" | custom-call | flops 4294967296 | bytes 8388608 | tf_op jit(solution)/shard_map/front/pallas_call | solution.py:173
  118.5 2.3 collective-permute-start.9
  120.8 1.3 collective-permute-start.10
  122.1 0.7 collective-permute-start.11
  122.8 1.3 collective-permute-start.6
  124.1 4.0 %collective-permute-start.7 = (bf16[2,4,8,2,16,128]{5,4,3,2,1,0:T(8,128)(2,1)}, bf16[2,4,8,2,16,128]{5,4,3,2,1,0:T(8,128)(2,1)}, u32[]{:S(2)}, u32[]{:S(2)}) collective-permute-start(bf16[2,4,8,2,16,128]{5,4,3,2,1,0:T(8,128)(2,1)} %get-tuple-element.56.refs_6_), channel_id=1, source_target_pairs={{0,4},{1,5},{2,6},{3,7},{4,8},{5,9},{6,10},{7,11},{16,20},{17,21},... | collective-permute-start | bytes 1572872 | tf_op jit(solution)/shard_map/ppermute | solution.py:422
  128.1 8.1 %collective-permute-done.9.refs_11_ = bf16[2,4,8,2,16,128]{5,4,3,2,1,0:T(8,128)(2,1)S(1)} collective-permute-done((bf16[2,4,8,2,16,128]{5,4,3,2,1,0:T(8,128)(2,1)}, bf16[2,4,8,2,16,128]{5,4,3,2,1,0:T(8,128)(2,1)S(1)}, u32[]{:S(2)}, u32[]{:S(2)}) %collective-permute-start.9) | collective-permute-done | bytes 524320 | tf_op jit(solution)/shard_map/ppermute | solution.py:422
  136.2 1.9 collective-permute-start.8
  138.1 9.4 %collective-permute-done.10.refs_12_ = bf16[2,4,8,2,16,128]{5,4,3,2,1,0:T(8,128)(2,1)S(1)} collective-permute-done((bf16[2,4,8,2,16,128]{5,4,3,2,1,0:T(8,128)(2,1)}, bf16[2,4,8,2,16,128]{5,4,3,2,1,0:T(8,128)(2,1)S(1)}, u32[]{:S(2)}, u32[]{:S(2)}) %collective-permute-start.10) | collective-permute-done | bytes 524320 | tf_op jit(solution)/shard_map/ppermute | solution.py:422
  147.5 1.5 collective-permute-done.7.refs_9_
  149.0 11.2 %collective-permute-done.8.refs_10_ = bf16[2,4,8,2,16,128]{5,4,3,2,1,0:T(8,128)(2,1)} collective-permute-done((bf16[2,4,8,2,16,128]{5,4,3,2,1,0:T(8,128)(2,1)}, bf16[2,4,8,2,16,128]{5,4,3,2,1,0:T(8,128)(2,1)}, u32[]{:S(2)}, u32[]{:S(2)}) %collective-permute-start.8) | collective-permute-done | bytes 524320 | tf_op jit(solution)/shard_map/ppermute | solution.py:422
  160.3 6.1 %meet.3 = (bf16[4,4,8,2,16,128]{5,4,3,2,1,0:T(8,128)(2,1)}, bf16[4,4,8,2,16,128]{5,4,3,2,1,0:T(8,128)(2,1)}, bf16[2,8,2,16,128]{4,3,2,1,0:T(8,128)(2,1)}, bf16[2...) custom-call(s32[2]{0:T(128)} %pad_add_fusion.1.where_ref, ...), custom_call_target="tpu_custom_call" | custom-call | flops 2621440 | bytes 10485760 | tf_op jit(solution)/shard_map/meet/pallas_call | solution.py:254
  166.4 30.3 %all_to_all.20.refs_1_ = bf16[16,8,2,16,128]{4,3,2,1,0:T(8,128)(2,1)} all-to-all(bf16[16,8,2,16,128]{4,3,2,1,0:T(8,128)(2,1)} %bitcast.12), channel_id=1, replica_groups=mesh['grp'=2,'chan'=16] {'chan'}, dimensions={0} | all-to-all | bytes 2097152 | tf_op jit(solution)/shard_map/all_to_all | solution.py:439
  196.7 4.9 %all-to-all-start.3 = ((bf16[16,8,2,16,128]{4,3,2,1,0:T(8,128)(2,1)}), bf16[16,8,2,16,128]{4,3,2,1,0:T(8,128)(2,1)S(1)}, u32[]{:S(2)}, u32[]{:S(2)}) async-start(bf16[16,8,2,16,128]{4,3,2,1,0:T(8,128)(2,1)} %bitcast.10), calls=%async_computation.3 | async-start | bytes 2097152 | tf_op jit(solution)/shard_map/all_to_all | solution.py:439
  201.6 0.6 collective-permute-start.15
  202.2 1.2 collective-permute-start.16
  203.4 0.1 rev.3
  203.5 0.6 copy.6
  204.1 1.3 mark.2.value_ref
  205.4 1.3 mark.3.order_ref
  206.6 1.7 collective-permute-start.12
  208.4 0.3 collective-permute-start.13
  208.6 0.2 collective-permute-done.15.refs_4_.refs_7_
  208.8 2.5 %collective-permute-start.14 = (bf16[1,8,2,16,128]{4,3,2,1,0:T(8,128)(2,1)S(1)}, bf16[1,8,2,16,128]{4,3,2,1,0:T(8,128)(2,1)S(1)}, u32[]{:S(2)}, u32[]{:S(2)}) collective-permute-start(bf16[1,8,2,16,128]{4,3,2,1,0:T(8,128)(2,1)S(1)} %copy-done.19), channel_id=1, source_target_pairs={{0,3},{1,0},{2,1},{3,2},{4,7},{5,4},{6,5},{7,6},{8,11},{9,8},{10,9... | collective-permute-start | bytes 196616 | tf_op jit(solution)/shard_map/ppermute | solution.py:485
  211.3 3.9 %collective-permute-done.16.refs_5_.refs_8_ = bf16[2,8,2,16,128]{4,3,2,1,0:T(8,128)(2,1)S(1)} collective-permute-done((bf16[2,8,2,16,128]{4,3,2,1,0:T(8,128)(2,1)}, bf16[2,8,2,16,128]{4,3,2,1,0:T(8,128)(2,1)S(1)}, u32[]{:S(2)}, u32[]{:S(2)}) %collective-permute-start.16) | collective-permute-done | bytes 131104 | tf_op jit(solution)/shard_map/ppermute | solution.py:485
  215.2 1.4 collective-permute-done.17.refs_6_.refs_9_
  216.6 0.6 copy-done.5
  217.3 13.2 %back.2.refs_10_ = bf16[16,1024,1024]{2,1,0:T(8,128)(2,1)} custom-call(s32[2]{0:T(128)} %pad_add_fusion.1.where_ref, s32[1,1024]{1,0:T(1,128)} %mark.3.order_ref, bf16[16,2,8,2,16,128]{5,4,3,2,1,0:T(8,128)(2,1)} %copy-done, bf16[16,8,2,16,128]{4,3,2,1,0:T(8,128)(2,1)} %all_to_all.20.refs_1_, bf16[16,2,8,2,16,128]{5,4,3,2,1,0:T(8,128)(2,1)} %copy-done, ...), custom_call_target="tpu_custom_call" | custom-call | flops 8589934592 | bytes 16777216 | tf_op jit(solution)/shard_map/back/pallas_call | solution.py:390
  230.5 0.6 copy-done.15
  231.1 0.0 copy-done.17
  231.1 0.4 copy-done.2
  231.5 13.1 %back.3 = bf16[16,1024,1024]{2,1,0:T(8,128)(2,1)} custom-call(s32[2]{0:T(128)} %pad_add_fusion.1.where_ref, s32[1,1024]{1,0:T(1,128)} %mark.3.order_ref, bf16[16,8,2,16,128]{4,3,2,1,0:T(8,128)(2,1)} %copy-done.1, bf16[16,8,2,16,128]{4,3,2,1,0:T(8,128)(2,1)} %copy-done.2, ...), custom_call_target="tpu_custom_call", output_to_operand_aliasing={{}: (12, {})} | custom-call | flops 8589934592 | bytes 16777216 | tf_op jit(solution)/shard_map/back/pallas_call | solution.py:390
  (56 shorter events, 0.1 us)
Async XLA Ops:
  21.5 61.9 %all-to-all-start = ((bf16[16,2,8,2,16,128]{5,4,3,2,1,0:T(8,128)(2,1)}), bf16[16,2,8,2,16,128]{5,4,3,2,1,0:T(8,128)(2,1)S(1)}, u32[]{:S(2)}, u32[]{:S(2)}) async-start(bf16[16,2,8,2,16,128]{5,4,3,2,1,0:T(8,128)(2,1)} %get-tuple-element.38), calls=%async_computation | async-start | bytes 4194304 | tf_op jit(solution)/shard_map/all_to_all | solution.py:439
  28.0 52.8 %collective-permute-start.3 = (bf16[1,4,8,2,16,128]{5,4,3,2,1,0:T(8,128)(2,1)}, bf16[1,4,8,2,16,128]{5,4,3,2,1,0:T(8,128)(2,1)S(1)}, u32[]{:S(2)}, u32[]{:S(2)}) collective-permute-start(bf16[1,4,8,2,16,128]{5,4,3,2,1,0:T(8,128)(2,1)} %get-tuple-element.39.refs_0_), channel_id=1, source_target_pairs={{4,0},{5,1},{6,2},{7,3},{8,4},{9,5},{10,6},{11,7},{12,8},{13,9},{1... | collective-permute-start | bytes 786440 | tf_op jit(solution)/shard_map/ppermute | solution.py:422
  30.2 56.2 %collective-permute-start.4 = (bf16[1,4,8,2,16,128]{5,4,3,2,1,0:T(8,128)(2,1)}, bf16[1,4,8,2,16,128]{5,4,3,2,1,0:T(8,128)(2,1)S(1)}, u32[]{:S(2)}, u32[]{:S(2)}) collective-permute-start(bf16[1,4,8,2,16,128]{5,4,3,2,1,0:T(8,128)(2,1)} %get-tuple-element.40.refs_1_), channel_id=1, source_target_pairs={{8,4},{9,5},{10,6},{11,7},{12,8},{13,9},{14,10},{15,11},{24,20},{2... | collective-permute-start | bytes 786440 | tf_op jit(solution)/shard_map/ppermute | solution.py:422
  31.5 54.9 %collective-permute-start.5 = (bf16[1,4,8,2,16,128]{5,4,3,2,1,0:T(8,128)(2,1)}, bf16[1,4,8,2,16,128]{5,4,3,2,1,0:T(8,128)(2,1)S(1)}, u32[]{:S(2)}, u32[]{:S(2)}) collective-permute-start(bf16[1,4,8,2,16,128]{5,4,3,2,1,0:T(8,128)(2,1)} %get-tuple-element.41.refs_2_), channel_id=1, source_target_pairs={{12,8},{13,9},{14,10},{15,11},{28,24},{29,25},{30,26},{31,27}} | collective-permute-start | bytes 786440 | tf_op jit(solution)/shard_map/ppermute | solution.py:422
  32.2 54.2 %collective-permute-start = (bf16[1,4,8,2,16,128]{5,4,3,2,1,0:T(8,128)(2,1)}, bf16[1,4,8,2,16,128]{5,4,3,2,1,0:T(8,128)(2,1)S(1)}, u32[]{:S(2)}, u32[]{:S(2)}) collective-permute-start(bf16[1,4,8,2,16,128]{5,4,3,2,1,0:T(8,128)(2,1)} %get-tuple-element.44.refs_5_), channel_id=1, source_target_pairs={{0,4},{1,5},{2,6},{3,7},{16,20},{17,21},{18,22},{19,23}} | collective-permute-start | bytes 786440 | tf_op jit(solution)/shard_map/ppermute | solution.py:422
  33.5 52.9 %collective-permute-start.1 = (bf16[1,4,8,2,16,128]{5,4,3,2,1,0:T(8,128)(2,1)}, bf16[1,4,8,2,16,128]{5,4,3,2,1,0:T(8,128)(2,1)S(1)}, u32[]{:S(2)}, u32[]{:S(2)}) collective-permute-start(bf16[1,4,8,2,16,128]{5,4,3,2,1,0:T(8,128)(2,1)} %get-tuple-element.45.refs_6_), channel_id=1, source_target_pairs={{0,4},{1,5},{2,6},{3,7},{4,8},{5,9},{6,10},{7,11},{16,20},{17,21},... | collective-permute-start | bytes 786440 | tf_op jit(solution)/shard_map/ppermute | solution.py:422
  80.8 8.5 %copy-start.10 = (bf16[1,4,8,2,16,128]{5,4,3,2,1,0:T(8,128)(2,1)}, bf16[1,4,8,2,16,128]{5,4,3,2,1,0:T(8,128)(2,1)S(1)}, u32[]{:S(2)}) copy-start(bf16[1,4,8,2,16,128]{5,4,3,2,1,0:T(8,128)(2,1)S(1)} %collective-permute-done.3.refs_11_) | copy-start | bytes 786436
  80.8 8.5 %collective-permute-start.2 = (bf16[1,4,8,2,16,128]{5,4,3,2,1,0:T(8,128)(2,1)}, bf16[1,4,8,2,16,128]{5,4,3,2,1,0:T(8,128)(2,1)}, u32[]{:S(2)}, u32[]{:S(2)}) collective-permute-start(bf16[1,4,8,2,16,128]{5,4,3,2,1,0:T(8,128)(2,1)} %get-tuple-element.46.refs_7_), channel_id=1, source_target_pairs={{0,4},{1,5},{2,6},{3,7},{4,8},{5,9},{6,10},{7,11},{8,12},{9,13},{1... | collective-permute-start | bytes 786440 | tf_op jit(solution)/shard_map/ppermute | solution.py:422
  83.4 35.0 %copy-start = (bf16[16,2,8,2,16,128]{5,4,3,2,1,0:T(8,128)(2,1)}, bf16[16,2,8,2,16,128]{5,4,3,2,1,0:T(8,128)(2,1)S(1)}, u32[]{:S(2)}) copy-start(bf16[16,2,8,2,16,128]{5,4,3,2,1,0:T(8,128)(2,1)S(1)} %all-to-all-done.refs_0_.refs_2_) | copy-start | bytes 6291460
  86.4 2.9 %copy-start.11 = (bf16[1,4,8,2,16,128]{5,4,3,2,1,0:T(8,128)(2,1)}, bf16[1,4,8,2,16,128]{5,4,3,2,1,0:T(8,128)(2,1)S(1)}, u32[]{:S(2)}) copy-start(bf16[1,4,8,2,16,128]{5,4,3,2,1,0:T(8,128)(2,1)S(1)} %collective-permute-done.4.refs_12_) | copy-start | bytes 786436
  86.4 2.9 %copy-start.12 = (bf16[1,4,8,2,16,128]{5,4,3,2,1,0:T(8,128)(2,1)}, bf16[1,4,8,2,16,128]{5,4,3,2,1,0:T(8,128)(2,1)S(1)}, u32[]{:S(2)}) copy-start(bf16[1,4,8,2,16,128]{5,4,3,2,1,0:T(8,128)(2,1)S(1)} %collective-permute-done.5.refs_13_) | copy-start | bytes 786436
  86.4 2.9 %copy-start.13 = (bf16[1,4,8,2,16,128]{5,4,3,2,1,0:T(8,128)(2,1)}, bf16[1,4,8,2,16,128]{5,4,3,2,1,0:T(8,128)(2,1)S(1)}, u32[]{:S(2)}) copy-start(bf16[1,4,8,2,16,128]{5,4,3,2,1,0:T(8,128)(2,1)S(1)} %collective-permute-done.refs_8_) | copy-start | bytes 786436
  86.4 2.9 %copy-start.14 = (bf16[1,4,8,2,16,128]{5,4,3,2,1,0:T(8,128)(2,1)}, bf16[1,4,8,2,16,128]{5,4,3,2,1,0:T(8,128)(2,1)S(1)}, u32[]{:S(2)}) copy-start(bf16[1,4,8,2,16,128]{5,4,3,2,1,0:T(8,128)(2,1)S(1)} %collective-permute-done.1.refs_9_) | copy-start | bytes 786436
  94.1 44.0 %all-to-all-start.1 = ((bf16[16,8,2,16,128]{4,3,2,1,0:T(8,128)(2,1)}), bf16[16,8,2,16,128]{4,3,2,1,0:T(8,128)(2,1)S(1)}, u32[]{:S(2)}, u32[]{:S(2)}) async-start(bf16[16,8,2,16,128]{4,3,2,1,0:T(8,128)(2,1)} %bitcast.11), calls=%async_computation.1 | async-start | bytes 2097152 | tf_op jit(solution)/shard_map/all_to_all | solution.py:439
  118.4 83.1 %copy-start.18 = (s32[1024]{0:T(1024)S(1)}, s32[1024]{0:T(1024)}, u32[]{:S(2)}) copy-start(s32[1024]{0:T(1024)} %param.7) | copy-start | bytes 12292
  118.4 88.2 %copy-start.21 = (bf16[1,8,2,16,128]{4,3,2,1,0:T(8,128)(2,1)S(1)}, bf16[1,8,2,16,128]{4,3,2,1,0:T(8,128)(2,1)}, u32[]{:S(2)}) copy-start(bf16[1,8,2,16,128]{4,3,2,1,0:T(8,128)(2,1)} %get-tuple-element.62) | copy-start | bytes 196612
  118.4 89.9 %copy-start.20 = (bf16[1,8,2,16,128]{4,3,2,1,0:T(8,128)(2,1)S(1)}, bf16[1,8,2,16,128]{4,3,2,1,0:T(8,128)(2,1)}, u32[]{:S(2)}) copy-start(bf16[1,8,2,16,128]{4,3,2,1,0:T(8,128)(2,1)} %get-tuple-element.63) | copy-start | bytes 196612
  118.5 90.4 %copy-start.19 = (bf16[1,8,2,16,128]{4,3,2,1,0:T(8,128)(2,1)S(1)}, bf16[1,8,2,16,128]{4,3,2,1,0:T(8,128)(2,1)}, u32[]{:S(2)}) copy-start(bf16[1,8,2,16,128]{4,3,2,1,0:T(8,128)(2,1)} %get-tuple-element.64) | copy-start | bytes 196612
  118.5 17.7 %collective-permute-start.9 = (bf16[2,4,8,2,16,128]{5,4,3,2,1,0:T(8,128)(2,1)}, bf16[2,4,8,2,16,128]{5,4,3,2,1,0:T(8,128)(2,1)S(1)}, u32[]{:S(2)}, u32[]{:S(2)}) collective-permute-start(bf16[2,4,8,2,16,128]{5,4,3,2,1,0:T(8,128)(2,1)} %get-tuple-element.50.refs_0_), channel_id=1, source_target_pairs={{4,0},{5,1},{6,2},{7,3},{8,4},{9,5},{10,6},{11,7},{12,8},{13,9},{1... | collective-permute-start | bytes 1572872 | tf_op jit(solution)/shard_map/ppermute | solution.py:422
  120.8 26.7 %collective-permute-start.10 = (bf16[2,4,8,2,16,128]{5,4,3,2,1,0:T(8,128)(2,1)}, bf16[2,4,8,2,16,128]{5,4,3,2,1,0:T(8,128)(2,1)S(1)}, u32[]{:S(2)}, u32[]{:S(2)}) collective-permute-start(bf16[2,4,8,2,16,128]{5,4,3,2,1,0:T(8,128)(2,1)} %get-tuple-element.51.refs_1_), channel_id=1, source_target_pairs={{8,4},{9,5},{10,6},{11,7},{12,8},{13,9},{14,10},{15,11},{24,20},{2... | collective-permute-start | bytes 1572872 | tf_op jit(solution)/shard_map/ppermute | solution.py:422
  122.1 25.4 %collective-permute-start.11 = (bf16[2,4,8,2,16,128]{5,4,3,2,1,0:T(8,128)(2,1)}, bf16[2,4,8,2,16,128]{5,4,3,2,1,0:T(8,128)(2,1)S(1)}, u32[]{:S(2)}, u32[]{:S(2)}) collective-permute-start(bf16[2,4,8,2,16,128]{5,4,3,2,1,0:T(8,128)(2,1)} %get-tuple-element.52.refs_2_), channel_id=1, source_target_pairs={{12,8},{13,9},{14,10},{15,11},{28,24},{29,25},{30,26},{31,27}} | collective-permute-start | bytes 1572872 | tf_op jit(solution)/shard_map/ppermute | solution.py:422
  122.8 24.7 %collective-permute-start.6 = (bf16[2,4,8,2,16,128]{5,4,3,2,1,0:T(8,128)(2,1)}, bf16[2,4,8,2,16,128]{5,4,3,2,1,0:T(8,128)(2,1)S(1)}, u32[]{:S(2)}, u32[]{:S(2)}) collective-permute-start(bf16[2,4,8,2,16,128]{5,4,3,2,1,0:T(8,128)(2,1)} %get-tuple-element.55.refs_5_), channel_id=1, source_target_pairs={{0,4},{1,5},{2,6},{3,7},{16,20},{17,21},{18,22},{19,23}} | collective-permute-start | bytes 1572872 | tf_op jit(solution)/shard_map/ppermute | solution.py:422
  124.1 24.9 %collective-permute-start.7 = (bf16[2,4,8,2,16,128]{5,4,3,2,1,0:T(8,128)(2,1)}, bf16[2,4,8,2,16,128]{5,4,3,2,1,0:T(8,128)(2,1)}, u32[]{:S(2)}, u32[]{:S(2)}) collective-permute-start(bf16[2,4,8,2,16,128]{5,4,3,2,1,0:T(8,128)(2,1)} %get-tuple-element.56.refs_6_), channel_id=1, source_target_pairs={{0,4},{1,5},{2,6},{3,7},{4,8},{5,9},{6,10},{7,11},{16,20},{17,21},... | collective-permute-start | bytes 1572872 | tf_op jit(solution)/shard_map/ppermute | solution.py:422
  136.2 24.1 %copy-start.6 = (bf16[2,4,8,2,16,128]{5,4,3,2,1,0:T(8,128)(2,1)}, bf16[2,4,8,2,16,128]{5,4,3,2,1,0:T(8,128)(2,1)S(1)}, u32[]{:S(2)}) copy-start(bf16[2,4,8,2,16,128]{5,4,3,2,1,0:T(8,128)(2,1)S(1)} %collective-permute-done.9.refs_11_) | copy-start | bytes 1572868
  136.2 24.1 %collective-permute-start.8 = (bf16[2,4,8,2,16,128]{5,4,3,2,1,0:T(8,128)(2,1)}, bf16[2,4,8,2,16,128]{5,4,3,2,1,0:T(8,128)(2,1)}, u32[]{:S(2)}, u32[]{:S(2)}) collective-permute-start(bf16[2,4,8,2,16,128]{5,4,3,2,1,0:T(8,128)(2,1)} %get-tuple-element.57.refs_7_), channel_id=1, source_target_pairs={{0,4},{1,5},{2,6},{3,7},{4,8},{5,9},{6,10},{7,11},{8,12},{9,13},{1... | collective-permute-start | bytes 1572872 | tf_op jit(solution)/shard_map/ppermute | solution.py:422
  138.1 92.4 %copy-start.1 = (bf16[16,8,2,16,128]{4,3,2,1,0:T(8,128)(2,1)}, bf16[16,8,2,16,128]{4,3,2,1,0:T(8,128)(2,1)S(1)}, u32[]{:S(2)}) copy-start(bf16[16,8,2,16,128]{4,3,2,1,0:T(8,128)(2,1)S(1)} %all-to-all-done.1.refs_0_) | copy-start | bytes 3145732
  147.5 12.8 %copy-start.7 = (bf16[2,4,8,2,16,128]{5,4,3,2,1,0:T(8,128)(2,1)}, bf16[2,4,8,2,16,128]{5,4,3,2,1,0:T(8,128)(2,1)S(1)}, u32[]{:S(2)}) copy-start(bf16[2,4,8,2,16,128]{5,4,3,2,1,0:T(8,128)(2,1)S(1)} %collective-permute-done.10.refs_12_) | copy-start | bytes 1572868
  147.5 12.8 %copy-start.8 = (bf16[2,4,8,2,16,128]{5,4,3,2,1,0:T(8,128)(2,1)}, bf16[2,4,8,2,16,128]{5,4,3,2,1,0:T(8,128)(2,1)S(1)}, u32[]{:S(2)}) copy-start(bf16[2,4,8,2,16,128]{5,4,3,2,1,0:T(8,128)(2,1)S(1)} %collective-permute-done.11.refs_13_) | copy-start | bytes 1572868
  147.5 12.8 %copy-start.9 = (bf16[2,4,8,2,16,128]{5,4,3,2,1,0:T(8,128)(2,1)}, bf16[2,4,8,2,16,128]{5,4,3,2,1,0:T(8,128)(2,1)S(1)}, u32[]{:S(2)}) copy-start(bf16[2,4,8,2,16,128]{5,4,3,2,1,0:T(8,128)(2,1)S(1)} %collective-permute-done.6.refs_8_) | copy-start | bytes 1572868
  196.7 33.9 %all-to-all-start.3 = ((bf16[16,8,2,16,128]{4,3,2,1,0:T(8,128)(2,1)}), bf16[16,8,2,16,128]{4,3,2,1,0:T(8,128)(2,1)S(1)}, u32[]{:S(2)}, u32[]{:S(2)}) async-start(bf16[16,8,2,16,128]{4,3,2,1,0:T(8,128)(2,1)} %bitcast.10), calls=%async_computation.3 | async-start | bytes 2097152 | tf_op jit(solution)/shard_map/all_to_all | solution.py:439
  201.6 7.2 %collective-permute-start.15 = (bf16[2,8,2,16,128]{4,3,2,1,0:T(8,128)(2,1)}, bf16[2,8,2,16,128]{4,3,2,1,0:T(8,128)(2,1)S(1)}, u32[]{:S(2)}, u32[]{:S(2)}) collective-permute-start(bf16[2,8,2,16,128]{4,3,2,1,0:T(8,128)(2,1)} %get-tuple-element.66), channel_id=1, source_target_pairs={{0,1},{1,2},{2,3},{3,0},{4,5},{5,6},{6,7},{7,4},{8,9},{9,10},{10,1... | collective-permute-start | bytes 393224 | tf_op jit(solution)/shard_map/ppermute | solution.py:485
  202.2 13.0 %collective-permute-start.16 = (bf16[2,8,2,16,128]{4,3,2,1,0:T(8,128)(2,1)}, bf16[2,8,2,16,128]{4,3,2,1,0:T(8,128)(2,1)S(1)}, u32[]{:S(2)}, u32[]{:S(2)}) collective-permute-start(bf16[2,8,2,16,128]{4,3,2,1,0:T(8,128)(2,1)} %get-tuple-element.67), channel_id=1, source_target_pairs={{0,2},{1,3},{2,0},{3,1},{4,6},{5,7},{6,4},{7,5},{8,10},{9,11},{10,... | collective-permute-start | bytes 393224 | tf_op jit(solution)/shard_map/ppermute | solution.py:485
  203.4 13.2 %collective-permute-start.17 = (bf16[2,8,2,16,128]{4,3,2,1,0:T(8,128)(2,1)}, bf16[2,8,2,16,128]{4,3,2,1,0:T(8,128)(2,1)S(1)}, u32[]{:S(2)}, u32[]{:S(2)}) collective-permute-start(bf16[2,8,2,16,128]{4,3,2,1,0:T(8,128)(2,1)} %get-tuple-element.68), channel_id=1, source_target_pairs={{0,3},{1,0},{2,1},{3,2},{4,7},{5,4},{6,5},{7,6},{8,11},{9,8},{10,9... | collective-permute-start | bytes 393224 | tf_op jit(solution)/shard_map/ppermute | solution.py:485
  206.6 23.8 %collective-permute-start.12 = (bf16[1,8,2,16,128]{4,3,2,1,0:T(8,128)(2,1)S(1)}, bf16[1,8,2,16,128]{4,3,2,1,0:T(8,128)(2,1)S(1)}, u32[]{:S(2)}, u32[]{:S(2)}) collective-permute-start(bf16[1,8,2,16,128]{4,3,2,1,0:T(8,128)(2,1)S(1)} %copy-done.21), channel_id=1, source_target_pairs={{0,1},{1,2},{2,3},{3,0},{4,5},{5,6},{6,7},{7,4},{8,9},{9,10},{10,1... | collective-permute-start | bytes 196616 | tf_op jit(solution)/shard_map/ppermute | solution.py:485
  208.4 22.1 %collective-permute-start.13 = (bf16[1,8,2,16,128]{4,3,2,1,0:T(8,128)(2,1)S(1)}, bf16[1,8,2,16,128]{4,3,2,1,0:T(8,128)(2,1)S(1)}, u32[]{:S(2)}, u32[]{:S(2)}) collective-permute-start(bf16[1,8,2,16,128]{4,3,2,1,0:T(8,128)(2,1)S(1)} %copy-done.20), channel_id=1, source_target_pairs={{0,2},{1,3},{2,0},{3,1},{4,6},{5,7},{6,4},{7,5},{8,10},{9,11},{10,... | collective-permute-start | bytes 196616 | tf_op jit(solution)/shard_map/ppermute | solution.py:485
  208.8 7.8 %copy-start.3 = (bf16[2,8,2,16,128]{4,3,2,1,0:T(8,128)(2,1)}, bf16[2,8,2,16,128]{4,3,2,1,0:T(8,128)(2,1)S(1)}, u32[]{:S(2)}) copy-start(bf16[2,8,2,16,128]{4,3,2,1,0:T(8,128)(2,1)S(1)} %collective-permute-done.15.refs_4_.refs_7_) | copy-start | bytes 393220
  208.8 21.7 %collective-permute-start.14 = (bf16[1,8,2,16,128]{4,3,2,1,0:T(8,128)(2,1)S(1)}, bf16[1,8,2,16,128]{4,3,2,1,0:T(8,128)(2,1)S(1)}, u32[]{:S(2)}, u32[]{:S(2)}) collective-permute-start(bf16[1,8,2,16,128]{4,3,2,1,0:T(8,128)(2,1)S(1)} %copy-done.19), channel_id=1, source_target_pairs={{0,3},{1,0},{2,1},{3,2},{4,7},{5,4},{6,5},{7,6},{8,11},{9,8},{10,9... | collective-permute-start | bytes 196616 | tf_op jit(solution)/shard_map/ppermute | solution.py:485
  215.2 1.4 copy-start.4
  216.6 0.7 copy-start.5
  230.5 0.6 copy-start.15
  230.5 0.6 copy-start.16
  230.5 0.6 copy-start.17
  230.5 1.0 copy-start.2
